TPU v7x, 32 devices: a whole 2x2x4 slice. The times are simulated.
32 devices in a mesh: head: 2 (over core), blk: 16 (over z, y, x).
Axes of the slice: x: 2, y: 2, z: 4, core: 2. Of those that a mesh axis runs over, the one named last changes fastest.
Arguments:
- tokens: bfloat16 [4096, 1536], P(('head', 'blk')), may hold values from -6 to 6
- lengths: int32 [12], replicated, may hold values from 1 to 2048, 4096 in all
- expert_ids: int32 [4096, 2], P(('head', 'blk')), may hold values from 0 to 15, all different within a row; in each aligned block of 128 rows (0 to 127, 128 to 255, ...) at most 48 rows name the same one
- w_query: bfloat16 [1536, 1536], P(('head', 'blk')), may hold values from -0.15625 to 0.15625
- w_key: bfloat16 [1536, 512], P(('head', 'blk')), may hold values from -0.15625 to 0.15625
- w_value: bfloat16 [1536, 512], P(('head', 'blk')), may hold values from -0.15625 to 0.15625
- w_out: bfloat16 [1536, 1536], P(('head', 'blk')), may hold values from -2.5 to 2.5
- w_router: bfloat16 [1536, 16], P(('head', 'blk')), may hold values from -0.15625 to 0.15625
- gain_attn: bfloat16 [1536], P(('head', 'blk')), may hold values from 0.5 to 1.5
- gain_moe: bfloat16 [1536], P(('head', 'blk')), may hold values from 0.5 to 1.5
- w_gate: bfloat16 [16, 1536, 1024], P('blk', None, 'head'), may hold values from -0.15625 to 0.15625
- w_up: bfloat16 [16, 1536, 1024], P('blk', None, 'head'), may hold values from -0.15625 to 0.15625
- w_down: bfloat16 [16, 1024, 1536], P('blk', 'head'), may hold values from -0.1875 to 0.1875
- cotangent: bfloat16 [4096, 1536], P(('head', 'blk')), may hold values from -6 to 6
Outputs:
- output: bfloat16 [4096, 1536], P(('head', 'blk'))
- input_grad: bfloat16 [4096, 1536], P(('head', 'blk'))
- grad_query: float32 [1536, 1536], P(('head', 'blk'))
- grad_key: float32 [1536, 512], P(('head', 'blk'))
- grad_value: float32 [1536, 512], P(('head', 'blk'))
- grad_out: float32 [1536, 1536], P(('head', 'blk'))
- grad_router: float32 [1536, 16], P(('head', 'blk'))
- grad_gain_attn: float32 [1536], P(('head', 'blk'))
- grad_gain_moe: float32 [1536], P(('head', 'blk'))
- grad_gate: float32 [16, 1536, 1024], P('blk', None, 'head')
- grad_up: float32 [16, 1536, 1024], P('blk', None, 'head')
- grad_down: float32 [16, 1024, 1536], P('blk', 'head')
Inputs may be any that keep to these rules, and one draw needn't show every extreme that they name: The last entry counts the padding tokens at the end of the token order; the others are the documents' lengths in order; all entries add up to 4096. `expert_ids`: each token names two different experts. Among the 128 tokens of one device no expert is named by more than 48 tokens, and some expert reaches that bound.
All inputs are finite; a program needn't handle non-finite values.
Results may differ from a plain program's by a relative error of at most 0.025.
Values may be sent and summed in bfloat16 or wider, within the bound.
No kernel may reach another device: no remote copies, remote signals or barrier semaphores. Data moves between devices by JAX's collectives and lax.ppermute only.
A program may use at most 256 MiB of HBM per device.

v0:
```python
import functools
import math

import jax
import jax.numpy as jnp
from jax import lax
from jax.experimental import pallas as pl
from jax.experimental.pallas import tpu as pltpu
from jax.sharding import Mesh
from jax.sharding import PartitionSpec as P


D = 1536
HQ = 24
HK = 8
HD = 64
GROUP = HQ // HK
QW = GROUP * HD
KV = 2 * HD
QKV = QW + KV
LANE = 128
EPS = 1e-05
NEG = -1e30
BQ = 128
KEYS = 256
WIDTHS = (3, 1)
WIDTHS_BACK = (2, 1)
F32 = jnp.float32
BF16 = jnp.bfloat16

TEAM = ("head", "hg")
BLK = ("hg", "tg")
ALL = ("head", "hg", "tg")


def pad_up(count):
    return -(-count // LANE) * LANE


def rms_scale(values):
    return lax.rsqrt(jnp.mean(values * values, axis=-1, keepdims=True) + EPS)


def doc_ranges(lengths_ref, segments, q_pos, first):
    start = jnp.zeros_like(q_pos)
    low = jnp.int32(0)
    end = jnp.int32(0)
    for j in range(segments):
        end = end + lengths_ref[j]
        start = jnp.where(q_pos >= end, end, start)
        low = jnp.where(first >= end, end, low)
    return start, low // KEYS


def head_rows(rows, h, shift):
    part = rows[:, h * HD : (h + 1) * HD]
    zero = jnp.zeros_like(part)
    return jnp.concatenate([zero, part] if shift else [part, zero], axis=1)


def dot_nt(a, b):
    return lax.dot_general(a, b, (((1,), (1,)), ((), ())), preferred_element_type=F32)


def dot_tn(a, b):
    return lax.dot_general(a, b, (((0,), (0,)), ((), ())), preferred_element_type=F32)


def key_place(block, parts, planes):
    first = block * parts
    return [((first + t) % planes, (first + t) // planes) for t in range(parts)]


def allowed_keys(block, start, q_pos):
    k_pos = block * KEYS + lax.broadcasted_iota(jnp.int32, (KEYS, BQ), 0)
    mask = (k_pos >= start) & (k_pos <= q_pos)
    return jnp.concatenate([mask] * GROUP, axis=1)


def in_widths(widths, low, high, visit, state):
    base = low
    for width in widths:
        turns = (high - base) // width
        state = lax.fori_loop(0, turns, functools.partial(visit, width, base), state)
        base = base + turns * width
    return state


def place_pieces(meta_ref, pieces, kv_ref):
    planes = len(pieces)
    for distance, piece in enumerate(pieces):
        kv_ref[(meta_ref[0] + planes - distance) % planes] = piece[...]


def attend_kernel(lengths_ref, meta_ref, q_ref, *refs, segments):
    pieces, (o_ref, lse_ref, kv_ref) = refs[:-3], refs[-3:]
    planes = kv_ref.shape[0]
    place_pieces(meta_ref, pieces, kv_ref)

    def one(step, carry):
        first = (step * planes + meta_ref[0]) * BQ
        rows = pl.ds(pl.multiple_of(step * BQ, BQ), BQ)
        q_pos = first + lax.broadcasted_iota(jnp.int32, (1, BQ), 1)
        start, low = doc_ranges(lengths_ref, segments, q_pos, first)
        high = (first + BQ - 1) // KEYS + 1
        q_part = q_ref[rows, :]
        queries = jnp.concatenate([head_rows(q_part, h, False) for h in range(GROUP)], axis=0)
        queries = queries * jnp.asarray(HD**-0.5, BF16)

        def visit(width, base, turn, state):
            run_max, run_sum, acc = state
            parts = []
            scores = []
            for u in range(width):
                block = base + turn * width + u
                places = key_place(block, KEYS // BQ, planes)
                part = jnp.concatenate([kv_ref[p, r] for p, r in places], axis=0)
                mask = allowed_keys(block, start, q_pos)
                parts.append(part[:, HD:])
                scores.append(jnp.where(mask, dot_nt(part, queries), NEG))
            new_max = run_max
            for value in scores:
                new_max = jnp.maximum(new_max, jnp.max(value, axis=0, keepdims=True))
            shrink = jnp.exp(run_max - new_max)
            run_sum = run_sum * shrink
            acc = acc * shrink
            for part, value in zip(parts, scores):
                weights = jnp.exp(value - new_max)
                run_sum = run_sum + jnp.sum(weights, axis=0, keepdims=True)
                acc = acc + dot_tn(part, weights.astype(BF16))
            return new_max, run_sum, acc

        begin = (
            jnp.full((1, GROUP * BQ), NEG, F32),
            jnp.zeros((1, GROUP * BQ), F32),
            jnp.zeros((HD, GROUP * BQ), F32),
        )
        top, total, acc = in_widths(WIDTHS, low, high, visit, begin)
        out = acc / total
        o_ref[rows, :] = jnp.concatenate(
            [out[:, h * BQ : (h + 1) * BQ] for h in range(GROUP)], axis=0
        ).T.astype(BF16)
        lse_ref[step] = top + jnp.log(total)
        return carry

    lax.fori_loop(0, q_ref.shape[0] // BQ, one, 0)


def attend_back_kernel(
    lengths_ref,
    meta_ref,
    q_ref,
    do_ref,
    o_ref,
    lse_ref,
    *refs,
    segments,
):
    planes = (len(refs) - 3) // 2
    pieces, dq_ref, sends = refs[:planes], refs[planes], refs[planes + 1 : 2 * planes + 1]
    kv_ref, acc_ref = refs[-2:]
    place_pieces(meta_ref, pieces, kv_ref)
    scale = HD**-0.5
    acc_ref[...] = jnp.zeros_like(acc_ref)

    def one(step, carry):
        first = (step * planes + meta_ref[0]) * BQ
        rows = pl.ds(pl.multiple_of(step * BQ, BQ), BQ)
        q_pos = first + lax.broadcasted_iota(jnp.int32, (1, BQ), 1)
        start, low = doc_ranges(lengths_ref, segments, q_pos, first)
        high = (first + BQ - 1) // KEYS + 1
        q_part = q_ref[rows, :]
        do_part = do_ref[rows, :]
        queries = jnp.concatenate([head_rows(q_part, h, False) for h in range(GROUP)], axis=0)
        queries = queries * jnp.asarray(scale, BF16)
        d_outs = jnp.concatenate([head_rows(do_part, h, True) for h in range(GROUP)], axis=0)
        products = (do_part.astype(F32) * o_ref[rows, :].astype(F32)).T
        row_dots = jnp.concatenate(
            [
                jnp.sum(products[h * HD : (h + 1) * HD], axis=0, keepdims=True)
                for h in range(GROUP)
            ],
            axis=1,
        )
        both = jnp.concatenate([queries, d_outs], axis=0)
        lse = lse_ref[step]

        def visit(width, base, turn, d_query):
            total = []
            for u in range(width):
                block = base + turn * width + u
                places = key_place(block, KEYS // BQ, planes)
                part = jnp.concatenate([kv_ref[p, r] for p, r in places], axis=0)
                mask = allowed_keys(block, start, q_pos)
                probs = jnp.where(mask, jnp.exp(dot_nt(part, queries) - lse), 0.0)
                d_scores = (probs * (dot_nt(part, d_outs) - row_dots)).astype(BF16)
                value = jnp.dot(
                    jnp.concatenate([d_scores, probs.astype(BF16)], axis=1),
                    both,
                    preferred_element_type=F32,
                )
                total.append((places, value))
                d_query = d_query + dot_tn(part[:, :HD], d_scores)
            for places, value in total:
                for t, (p, r) in enumerate(places):
                    acc_ref[p, r] += value[t * BQ : (t + 1) * BQ]
            return d_query

        begin = jnp.zeros((HD, GROUP * BQ), F32)
        d_query = in_widths(WIDTHS_BACK, low, high, visit, begin) * scale
        dq_ref[rows, :] = jnp.concatenate(
            [d_query[:, h * BQ : (h + 1) * BQ] for h in range(GROUP)], axis=0
        ).T.astype(BF16)
        return carry

    lax.fori_loop(0, q_ref.shape[0] // BQ, one, 0)
    for distance, send in enumerate(sends):
        send[...] = acc_ref[(meta_ref[0] + distance) % planes].astype(BF16)


def vmem_specs(count):
    return [pl.BlockSpec(memory_space=pltpu.SMEM)] * 2 + [
        pl.BlockSpec(memory_space=pltpu.VMEM)
    ] * count


def attend(lengths, meta, query, pieces):
    rows = query.shape[0]
    whole = (len(pieces),) + pieces[0].shape
    return pl.pallas_call(
        functools.partial(attend_kernel, segments=lengths.shape[0]),
        out_shape=(
            jax.ShapeDtypeStruct((rows, QW), BF16),
            jax.ShapeDtypeStruct((rows // BQ, 1, GROUP * BQ), F32),
        ),
        in_specs=vmem_specs(1 + len(pieces)),
        scratch_shapes=[pltpu.VMEM(whole, BF16)],
        compiler_params=pltpu.CompilerParams(
            vmem_limit_bytes=math.prod(whole) * 6 + (10 << 20)
        ),
        name="attend",
    )(lengths, meta, query, *pieces)


def attend_back(lengths, meta, query, d_out, out, lse, pieces):
    rows = query.shape[0]
    whole = (len(pieces),) + pieces[0].shape
    send = jax.ShapeDtypeStruct(pieces[0].shape, BF16)
    return pl.pallas_call(
        functools.partial(attend_back_kernel, segments=lengths.shape[0]),
        out_shape=(jax.ShapeDtypeStruct((rows, QW), BF16),) + (send,) * len(pieces),
        in_specs=vmem_specs(4 + len(pieces)),
        scratch_shapes=[pltpu.VMEM(whole, BF16), pltpu.VMEM(whole, F32)],
        compiler_params=pltpu.CompilerParams(
            vmem_limit_bytes=math.prod(whole) * 14 + (10 << 20)
        ),
        name="attend_back",
    )(lengths, meta, query, d_out, out, lse, *pieces)


def project_kernel(place_ref, *refs, members):
    pieces = refs[: 2 * (2 * members - 1)]
    slab_ref, normed_ref, q_ref, kv_ref, weight_ref, gain_ref, x_ref, sems = refs[len(pieces) :]
    planes, team, rows, _ = slab_ref.shape
    member, head = place_ref[0], place_ref[1]
    copies = []
    for side in range(2):
        for shift in range(1 - members, members):
            index = len(copies)
            block = member + shift
            fits = (block >= 0) & (block < members)
            row = jnp.clip(jnp.abs(side - head) * members + block, 0, team - 1) * BQ
            copy = pltpu.make_async_copy(
                pieces[index], x_ref.at[pl.ds(pl.multiple_of(row, BQ), BQ), :], sems.at[index]
            )
            copies.append((fits, copy))
    for fits, copy in copies:
        pl.when(fits)(copy.start)
    for g in range(team):
        for p in range(planes):
            at = (g * planes + p) * rows
            weight_ref[at : at + rows, :] = slab_ref[p, g]
    low = QKV // LANE * LANE
    side = weight_ref[:, low : low + LANE].astype(F32).T
    gain_ref[...] = side[QKV - low : QKV - low + 1]
    for fits, copy in copies:
        pl.when(fits)(copy.wait)

    def one(step, carry):
        block = chunk_of(step, BQ)
        x = x_ref[block, :].astype(F32)
        normed = (x * rms_scale(x) * gain_ref[...]).astype(BF16)
        normed_ref[block, :] = normed
        qkv = jnp.dot(normed, weight_ref[...], preferred_element_type=F32).astype(BF16)
        q_ref[block, :] = qkv[:, :QW]
        kv_ref[block, :] = qkv[:, QW:QKV]
        return carry

    lax.fori_loop(0, x_ref.shape[0] // BQ, one, 0)


def project(place, pieces, slab, members):
    planes, team, _, width = slab.shape
    rows = team * BQ
    return pl.pallas_call(
        functools.partial(project_kernel, members=members),
        out_shape=(
            jax.ShapeDtypeStruct((rows, D), BF16),
            jax.ShapeDtypeStruct((rows, QW), BF16),
            jax.ShapeDtypeStruct((rows, KV), BF16),
            jax.ShapeDtypeStruct((D, width), BF16),
            jax.ShapeDtypeStruct((1, D), F32),
        ),
        in_specs=[pl.BlockSpec(memory_space=pltpu.SMEM)]
        + [pl.BlockSpec(memory_space=pltpu.HBM)] * len(pieces)
        + [pl.BlockSpec(memory_space=pltpu.VMEM)],
        scratch_shapes=[
            pltpu.VMEM((rows, D), BF16),
            pltpu.SemaphoreType.DMA((len(pieces),)),
        ],
        compiler_params=pltpu.CompilerParams(vmem_limit_bytes=planes * rows * KV * 4 + (16 << 20)),
        name="project",
    )(place, *pieces, slab)


def line_gather(rows, members, partner):
    own = {0: rows}
    other = {}
    up = down = rows
    other[0] = lax.ppermute(rows, "head", partner)
    last = members - 1
    for turn in range(last):
        up = lax.ppermute(up, "hg", [(m, m + 1) for m in range(turn, last)])
        down = lax.ppermute(down, "hg", [(m, m - 1) for m in range(last - turn, 0, -1)])
        up, down = lax.optimization_barrier((up, down))
        own[-1 - turn], own[1 + turn] = up, down
        other[-1 - turn] = lax.ppermute(up, "head", partner)
        other[1 + turn] = lax.ppermute(down, "head", partner)
    order = range(-last, members)
    return [own[k] for k in order] + [other[k] for k in order]


def chunk_of(index, width):
    return pl.ds(pl.multiple_of(index * width, width), width)


def grad_in_kernel(normed_ref, qkv_ref, extras_ref, out_ref):
    planes, _, rows, width = out_ref.shape
    step = D // 4
    owners = step // rows
    low = width - extras_ref.shape[1]

    def one(index, carry):
        part = chunk_of(index, step)
        value = dot_tn(normed_ref[:, part], qkv_ref[...])
        value = jnp.concatenate([value[:, :low], value[:, low:] + extras_ref[part, :]], axis=1)
        value = value.astype(BF16)
        for k in range(owners):
            owner = index * owners + k
            out_ref[owner % planes, owner // planes] = value[k * rows : (k + 1) * rows]
        return carry

    lax.fori_loop(0, D // step, one, 0)


def grad_in_parts(normed, d_qkv, extras, planes, team):
    rows = D // (planes * team)
    width = d_qkv.shape[1]
    return pl.pallas_call(
        grad_in_kernel,
        out_shape=jax.ShapeDtypeStruct((planes, team, rows, width), BF16),
        compiler_params=pltpu.CompilerParams(vmem_limit_bytes=16 << 20),
        name="grad_in",
    )(normed, d_qkv, extras)


def attn_back_kernel(proj_ref, full_ref, out_ref):
    step = 3 * LANE

    def one(index, carry):
        part = chunk_of(index, step)
        out_ref[:, part] = dot_nt(proj_ref[...], full_ref[part, :D]).astype(BF16)
        return carry

    lax.fori_loop(0, D // step, one, 0)


def attn_back(d_proj, full_out):
    return pl.pallas_call(
        attn_back_kernel,
        out_shape=jax.ShapeDtypeStruct(d_proj.shape, BF16),
        compiler_params=pltpu.CompilerParams(vmem_limit_bytes=10 << 20),
        name="attn_back",
    )(d_proj, full_out)


def side_columns(shape, expert, experts):
    column = lax.broadcasted_iota(jnp.int32, shape, 1)
    return column == expert, column == expert + experts


def expert_kernel(
    expert_ref,
    x_own_ref,
    x_other_ref,
    d_own_ref,
    d_other_ref,
    gate_ref,
    up_ref,
    down_ref,
    back_ref,
    inner_ref,
    d_gate_ref,
    d_up_ref,
    x_ref,
    d_ref,
    sems,
    *,
    experts,
):
    slots = x_own_ref.shape[0]
    pairs = (
        (x_own_ref, x_ref.at[:slots]),
        (x_other_ref, x_ref.at[slots:]),
        (d_own_ref, d_ref.at[:slots]),
        (d_other_ref, d_ref.at[slots:]),
    )
    copies = [
        pltpu.make_async_copy(source, target, sems.at[index])
        for index, (source, target) in enumerate(pairs)
    ]
    for copy in copies:
        copy.start()
    for copy in copies:
        copy.wait()
    half = gate_ref.shape[1] // 2

    def rows_of(turn, carry):
        block = chunk_of(turn, slots)
        side = x_ref[block, D:].astype(F32)
        high, low = side_columns(side.shape, expert_ref[0], experts)
        mix = jnp.sum(jnp.where(high | low, side, 0.0), axis=1, keepdims=True)

        def units_of(index, d_mix):
            part = chunk_of(index, half)
            x = x_ref[block, :D]
            gate = jnp.dot(x, gate_ref[:, part], preferred_element_type=F32)
            up = jnp.dot(x, up_ref[:, part], preferred_element_type=F32)
            d_inner = dot_nt(d_ref[block, :], down_ref[part, :])
            sigmoid = jax.nn.sigmoid(gate)
            act = gate * sigmoid
            inner = act * up
            d_mix = d_mix + jnp.sum(d_inner * inner, axis=1, keepdims=True)
            d_inner = d_inner * mix
            inner_ref[block, part] = (inner * mix).astype(BF16)
            d_gate_ref[block, part] = (
                d_inner * up * sigmoid * (1.0 + gate * (1.0 - sigmoid))
            ).astype(BF16)
            d_up_ref[block, part] = (d_inner * act).astype(BF16)
            return d_mix

        d_mix = lax.fori_loop(0, 2, units_of, jnp.zeros((slots, 1), F32))

        def columns_of(index, carry):
            part = chunk_of(index, D // 3)
            back_ref[block, part] = (
                dot_nt(d_gate_ref[block, :], gate_ref[part, :])
                + dot_nt(d_up_ref[block, :], up_ref[part, :])
            ).astype(BF16)
            return carry

        lax.fori_loop(0, 3, columns_of, 0)
        d_high, d_low = split_float(d_mix)
        back_ref[block, D:] = jnp.where(
            high, d_high.astype(F32), jnp.where(low, d_low.astype(F32), 0.0)
        ).astype(BF16)
        return carry

    lax.fori_loop(0, 2, rows_of, 0)


def visit_expert(expert, x_own, x_other, d_own, d_other, gate, up, down, experts):
    slots, width = x_own.shape
    inner = jax.ShapeDtypeStruct((2 * slots, gate.shape[1]), BF16)
    return pl.pallas_call(
        functools.partial(expert_kernel, experts=experts),
        out_shape=(jax.ShapeDtypeStruct((2 * slots, width), BF16), inner, inner, inner),
        in_specs=[pl.BlockSpec(memory_space=pltpu.SMEM)]
        + [pl.BlockSpec(memory_space=pl.ANY)] * 4
        + [pl.BlockSpec(memory_space=pltpu.VMEM)] * 3,
        scratch_shapes=[
            pltpu.VMEM((2 * slots, width), BF16),
            pltpu.VMEM((2 * slots, D), BF16),
            pltpu.SemaphoreType.DMA((4,)),
        ],
        compiler_params=pltpu.CompilerParams(vmem_limit_bytes=26 << 20),
        name="expert",
    )(expert, x_own, x_other, d_own, d_other, gate, up, down)


def pair_kernel(expert_ref, own_ref, other_ref, out_ref, *, experts):
    total = own_ref[...].astype(F32) + other_ref[...].astype(F32)
    out_ref[:, :D] = total[:, :D].astype(BF16)
    side = total[:, D:]
    d_high, d_low = split_float(jnp.sum(side, axis=1, keepdims=True))
    high, low = side_columns(side.shape, expert_ref[0], experts)
    out_ref[:, D:] = jnp.where(
        high, d_high.astype(F32), jnp.where(low, d_low.astype(F32), 0.0)
    ).astype(BF16)


def pair_back(expert, partial, theirs, experts):
    slots, width = theirs.shape
    step = slots // 4
    return pl.pallas_call(
        functools.partial(pair_kernel, experts=experts),
        grid=(slots // step,),
        out_shape=jax.ShapeDtypeStruct((slots, width), BF16),
        in_specs=[
            pl.BlockSpec(memory_space=pltpu.SMEM),
            pl.BlockSpec((step, width), lambda i: (i, 0)),
            pl.BlockSpec((step, width), lambda i: (i, 0)),
        ],
        out_specs=pl.BlockSpec((step, width), lambda i: (i, 0)),
        compiler_params=pltpu.CompilerParams(vmem_limit_bytes=8 << 20),
        name="pair_back",
    )(expert, partial, theirs)


def expert_grads_kernel(
    x_own_ref,
    x_other_ref,
    d_own_ref,
    d_other_ref,
    inner_ref,
    d_gate_ref,
    d_up_ref,
    gate_ref,
    up_ref,
    down_ref,
):
    x = jnp.concatenate([x_own_ref[...], x_other_ref[...]], axis=0)
    d = jnp.concatenate([d_own_ref[...], d_other_ref[...]], axis=0)
    gate_ref[0] = dot_tn(x, d_gate_ref[...])
    up_ref[0] = dot_tn(x, d_up_ref[...])
    down_ref[0] = dot_tn(inner_ref[...], d)


def expert_grads(x_own, x_other, d_own, d_other, inner, d_gate, d_up):
    slots = x_own.shape[0]
    width = inner.shape[1]
    step = LANE
    part = pl.BlockSpec((slots, step), lambda i: (0, i))
    whole = pl.BlockSpec(inner.shape, lambda i: (0, 0))
    return pl.pallas_call(
        expert_grads_kernel,
        grid=(D // step,),
        out_shape=(
            jax.ShapeDtypeStruct((1, D, width), F32),
            jax.ShapeDtypeStruct((1, D, width), F32),
            jax.ShapeDtypeStruct((1, width, D), F32),
        ),
        in_specs=[part] * 4 + [whole] * 3,
        out_specs=[
            pl.BlockSpec((1, step, width), lambda i: (0, i, 0)),
            pl.BlockSpec((1, step, width), lambda i: (0, i, 0)),
            pl.BlockSpec((1, width, step), lambda i: (0, 0, i)),
        ],
        compiler_params=pltpu.CompilerParams(vmem_limit_bytes=24 << 20),
        name="expert_grads",
    )(x_own, x_other, d_own, d_other, inner, d_gate, d_up)


def row_of(weights, values):
    return lax.dot_general(
        weights,
        values,
        (((1,), (1,)), ((), ())),
        precision=lax.Precision.HIGHEST,
        preferred_element_type=F32,
    )[:1]


def finish_kernel(parts_ref, slab_ref, q_ref, k_ref, v_ref, router_ref, attn_ref, moe_ref):
    rows, experts = router_ref.shape
    width = slab_ref.shape[2] - QKV

    def two_groups(index, carry):
        small, along = carry
        parts = [parts_ref[2 * index + k].astype(F32) for k in range(2)]
        q_ref[:, chunk_of(index, 2 * QW)] = jnp.concatenate([p[:, :QW] for p in parts], axis=1)
        for ref, at in ((k_ref, QW), (v_ref, QW + HD)):
            ref[:, chunk_of(index, 2 * HD)] = jnp.concatenate(
                [p[:, at : at + HD] for p in parts], axis=1
            )
        for k, part in enumerate(parts):
            along = along + part[:, :QKV] * slab_ref[2 * index + k, :, :QKV].astype(F32)
            small = small + part[:, QKV:]
        return small, along

    begin = (jnp.zeros((rows, width), F32), jnp.zeros((rows, QKV), F32))
    small, along = lax.fori_loop(0, HK // 2, two_groups, begin)
    router_ref[...] = small[:, :experts]
    column = lax.broadcasted_iota(jnp.int32, (8, width), 1)
    moe_ref[...] = row_of((column == experts).astype(F32), small)
    gain = row_of((column == 0).astype(F32), slab_ref[0, :, QKV:].astype(F32))
    attn_ref[...] = row_of(jnp.ones((8, QKV), F32), along) / gain


def finish_grads(parts, by_group, experts):
    rows = by_group.shape[1]

    def shape(columns):
        return jax.ShapeDtypeStruct((rows, columns), F32)

    line = jax.ShapeDtypeStruct((1, rows), F32)
    out = pl.pallas_call(
        finish_kernel,
        out_shape=(
            shape(HQ * HD),
            shape(HK * HD),
            shape(HK * HD),
            shape(experts),
            line,
            line,
        ),
        compiler_params=pltpu.CompilerParams(vmem_limit_bytes=8 << 20),
        name="finish_grads",
    )(parts, by_group)
    return out[:4] + (out[4].reshape(rows), out[5].reshape(rows))


def slab_rows(qkv_ref, slab_ref, out_ref, turn):
    def one(index, carry):
        source = chunk_of(turn * (out_ref.shape[0] // (2 * BQ)) + index, 2 * BQ)
        out_ref[chunk_of(index, 2 * BQ), :] = dot_nt(qkv_ref[source, :], slab_ref[...]).astype(BF16)
        return carry

    lax.fori_loop(0, out_ref.shape[0] // (2 * BQ), one, 0)


def merge_kernel(turn_ref, dq_ref, *refs):
    parts, (slab_ref, qkv_ref, out_ref) = refs[:-3], refs[-3:]
    zero = jnp.zeros((2 * BQ, qkv_ref.shape[1] - QKV), BF16)

    def one(index, carry):
        rows = chunk_of(index, 2 * BQ)
        d_kv = sum(part[rows, :].astype(F32) for part in parts).astype(BF16)
        qkv_ref[rows, :] = jnp.concatenate([dq_ref[rows, :], d_kv, zero], axis=1)
        return carry

    lax.fori_loop(0, dq_ref.shape[0] // (2 * BQ), one, 0)
    slab_rows(qkv_ref, slab_ref, out_ref, turn_ref[0])


def merge_back(turn, d_query, d_kv_parts, slab, heads):
    rows = d_query.shape[0]
    planes = len(d_kv_parts)
    return pl.pallas_call(
        merge_kernel,
        out_shape=(
            jax.ShapeDtypeStruct((rows, slab.shape[1]), BF16),
            jax.ShapeDtypeStruct((rows // heads, D), BF16),
        ),
        in_specs=[pl.BlockSpec(memory_space=pltpu.SMEM)]
        + [pl.BlockSpec(memory_space=pltpu.VMEM)] * (planes + 2),
        compiler_params=pltpu.CompilerParams(vmem_limit_bytes=planes * rows * KV * 4 + (12 << 20)),
        name="merge_back",
    )(turn, d_query, *d_kv_parts, slab)


def slab_back_kernel(turn_ref, qkv_ref, slab_ref, out_ref):
    slab_rows(qkv_ref, slab_ref, out_ref, turn_ref[0])


def slab_back(turn, d_qkv, slab, heads):
    return pl.pallas_call(
        slab_back_kernel,
        out_shape=jax.ShapeDtypeStruct((d_qkv.shape[0] // heads, D), BF16),
        in_specs=[
            pl.BlockSpec(memory_space=pltpu.SMEM),
            pl.BlockSpec(memory_space=pltpu.VMEM),
            pl.BlockSpec(memory_space=pltpu.VMEM),
        ],
        compiler_params=pltpu.CompilerParams(vmem_limit_bytes=10 << 20),
        name="slab_back",
    )(turn, d_qkv, slab)


def line_sum(parts, place):
    last = parts.shape[0] - 1
    up = jnp.zeros(parts.shape[1:], BF16)
    down = jnp.zeros(parts.shape[1:], BF16)

    def block(index):
        return lax.dynamic_index_in_dim(parts, jnp.clip(index, 0, last), 0, keepdims=False)

    for turn in range(last):
        to_up = block(place + last - turn)
        to_down = block(place - last + turn)
        if turn:
            to_up = (to_up.astype(F32) + up.astype(F32)).astype(BF16)
            to_down = (to_down.astype(F32) + down.astype(F32)).astype(BF16)
        up = lax.ppermute(to_up, "hg", [(m, m + 1) for m in range(turn + 1)])
        down = lax.ppermute(to_down, "hg", [(m, m - 1) for m in range(last, last - turn - 1, -1)])
        up, down = lax.optimization_barrier((up, down))
    return block(place).astype(F32) + up.astype(F32) + down.astype(F32)


def split_float(value):
    high = value.astype(BF16)
    return high, (value - high.astype(F32)).astype(BF16)


def shards(
    tokens,
    lengths,
    expert_ids,
    w_query,
    w_key,
    w_value,
    w_out,
    w_router,
    gain_attn,
    gain_moe,
    w_gate,
    w_up,
    w_down,
    cotangent,
):
    heads = lax.axis_size("head")
    planes = lax.axis_size("tg")
    members = lax.axis_size("hg")
    blk_count = planes * members
    in_group = heads * members
    tok_dev = tokens.shape[0]
    rows_dev = w_query.shape[0]
    experts = blk_count
    capacity = max(2, 3 * tok_dev // experts)
    slots = experts * capacity
    rows_group = in_group * tok_dev
    slab = pad_up(QKV + experts + 1)
    plane = lax.axis_index("tg")
    member = lax.axis_index("hg")
    blk_index = member * planes + plane
    partner = [(i, heads - 1 - i) for i in range(heads)]

    by_group = jnp.concatenate(
        [
            w_query.reshape(rows_dev, in_group, QW),
            w_key.reshape(rows_dev, in_group, HD),
            w_value.reshape(rows_dev, in_group, HD),
            jnp.broadcast_to(gain_attn[:, None, None], (rows_dev, in_group, 1)),
            jnp.zeros((rows_dev, in_group, slab - QKV - 1), BF16),
        ],
        axis=2,
    ).transpose(1, 0, 2)
    slab_team = lax.all_to_all(
        by_group, TEAM, split_axis=0, concat_axis=0, tiled=True
    )
    own_slab = lax.all_to_all(
        jnp.broadcast_to(slab_team[None], (planes, in_group, rows_dev, slab)),
        "tg",
        split_axis=0,
        concat_axis=0,
        tiled=True,
    )
    pieces = line_gather(tokens, members, partner)
    out_shard = jnp.concatenate(
        [
            w_out,
            w_router,
            gain_moe[:, None],
            jnp.zeros((rows_dev, pad_up(experts + 1) - experts - 1), BF16),
        ],
        axis=1,
    )
    full_out = lax.all_gather(out_shard, ALL, axis=0, tiled=True)

    seq_ends = jnp.cumsum(lengths)
    own_pos = (lax.axis_index("head") * blk_count + blk_index) * tok_dev + jnp.arange(
        tok_dev, dtype=jnp.int32
    )
    valid_bool = own_pos < seq_ends[-2]
    valid_float = valid_bool.astype(F32)[:, None]
    expert_range = jnp.arange(experts, dtype=jnp.int32)
    pair_experts = expert_ids.reshape(-1)
    live_pairs = jnp.repeat(valid_bool, 2)
    onehot = (
        (pair_experts[:, None] == expert_range[None, :]) & live_pairs[:, None]
    ).astype(jnp.int32)
    earlier = jnp.cumsum(onehot, axis=0) - onehot
    slot_index = jnp.sum(earlier * onehot, axis=1)
    kept_pairs = live_pairs & (slot_index < capacity)
    flat_index = jnp.where(kept_pairs, pair_experts * capacity + slot_index, -1)
    slot_ids = jnp.arange(slots, dtype=jnp.int32)
    token_index = flat_index.reshape(tok_dev, 2)
    token_table = (
        (token_index[:, 0][:, None] == slot_ids[None, :])
        | (token_index[:, 1][:, None] == slot_ids[None, :])
    ).astype(BF16)
    picked = (expert_ids[:, 0][:, None] == expert_range[None, :]) | (
        expert_ids[:, 1][:, None] == expert_range[None, :]
    )
    side = pad_up(2 * experts)
    side_zeros = jnp.zeros((tok_dev, side - 2 * experts), BF16)

    def exchange(rows):
        return lax.all_to_all(
            rows.reshape(experts, capacity, rows.shape[1]),
            BLK,
            split_axis=0,
            concat_axis=0,
            tiled=True,
        ).reshape(slots, rows.shape[1])

    def pick_rows(values):
        return lax.dot_general(
            token_table, values, (((0,), (0,)), ((), ())), preferred_element_type=F32
        ).astype(BF16)

    normed_one, query, kv_own, own_slab, gain_one = project(
        jnp.stack([member, lax.axis_index("head")]).astype(jnp.int32),
        pieces,
        own_slab,
        members,
    )

    def next_planes(distance):
        return [(p, (p + distance) % planes) for p in range(planes)]

    kv_own = kv_own.reshape(in_group, tok_dev, KV)
    kv_pieces = [kv_own] + [
        lax.ppermute(kv_own, "tg", next_planes(distance)) for distance in range(1, planes)
    ]
    d_send = pick_rows(cotangent)
    d_sent = exchange(d_send)
    meta = plane.astype(jnp.int32).reshape(1)
    attn_rows, lse = attend(lengths, meta, query, kv_pieces)
    d_sent, attn_rows = lax.optimization_barrier((d_sent, attn_rows))
    attn_tokens = lax.all_to_all(attn_rows, TEAM, split_axis=0, concat_axis=1, tiled=True)

    own_x = tokens.astype(F32)
    hidden_one = own_x + jnp.dot(attn_tokens, full_out[:, :D], preferred_element_type=F32)
    scale_two = rms_scale(hidden_one)
    gain_two = full_out[:, D + experts].astype(F32)[None, :]
    router = full_out[:, D : D + experts]
    normed_two = (hidden_one * scale_two * gain_two).astype(BF16)
    logits = jnp.dot(normed_two, router, preferred_element_type=F32)
    mix = jax.nn.softmax(jnp.where(picked, logits, NEG), axis=1)
    mix_high, mix_low = split_float(mix)
    moe_send = pick_rows(jnp.concatenate([normed_two, mix_high, mix_low, side_zeros], axis=1))
    moe_sent = exchange(moe_send)
    moe_other = lax.ppermute(moe_sent, "head", partner)
    d_other = lax.ppermute(d_sent, "head", partner)

    down_mat = w_down[0]
    expert = blk_index.astype(jnp.int32).reshape(1)
    partial, inner_mixed, d_gate, d_up = visit_expert(
        expert, moe_sent, moe_other, d_sent, d_other, w_gate[0], w_up[0], down_mat, experts
    )
    summed = pair_back(
        expert, partial, lax.ppermute(partial[slots:], "head", partner), experts
    )
    d_back = exchange(summed)
    y_part = jnp.dot(inner_mixed, down_mat, preferred_element_type=F32)
    y_theirs = lax.ppermute(y_part[slots:].astype(BF16), "head", partner)
    y_send = (y_part[:slots] + y_theirs.astype(F32)).astype(BF16)
    grad_gate, grad_up, grad_down = expert_grads(
        moe_sent, moe_other, d_sent, d_other, inner_mixed, d_gate, d_up
    )

    d_out = cotangent.astype(F32) * valid_float
    d_token = jnp.dot(token_table, d_back, preferred_element_type=F32)
    d_mix = d_token[:, D : D + experts] + d_token[:, D + experts : D + 2 * experts]
    d_logits = (mix * (d_mix - jnp.sum(mix * d_mix, axis=1, keepdims=True))).astype(BF16)
    grad_router_part = jnp.einsum("td,te->de", normed_two, d_logits, preferred_element_type=F32)
    d_normed_two = d_token[:, :D] + jnp.einsum(
        "te,de->td", d_logits, router, preferred_element_type=F32
    )
    gain_moe_part = lax.dot_general(
        d_normed_two * hidden_one,
        scale_two,
        (((0,), (0,)), ((), ())),
        precision=lax.Precision.HIGHEST,
        preferred_element_type=F32,
    )
    extras = jnp.pad(
        jnp.concatenate([grad_router_part, gain_moe_part], axis=1),
        ((0, 0), (QKV % LANE, slab - QKV - experts - 1)),
    )
    along_two = gain_two * d_normed_two
    d_hidden = (
        d_out
        + scale_two * along_two
        - hidden_one
        * (
            scale_two
            * scale_two
            * scale_two
            * jnp.mean(along_two * hidden_one, axis=-1, keepdims=True)
        )
    )
    d_proj = d_hidden.astype(BF16)
    d_attn = attn_back(d_proj, full_out)
    d_attn_rows = lax.all_to_all(d_attn, TEAM, split_axis=1, concat_axis=0, tiled=True)
    d_attn_rows, y_send = lax.optimization_barrier((d_attn_rows, y_send))
    y_back = exchange(y_send)
    d_query, *d_kv_sends = attend_back(lengths, meta, query, d_attn_rows, attn_rows, lse, kv_pieces)
    d_proj, d_query = lax.optimization_barrier((d_proj, d_query))
    d_proj_group = lax.all_gather(d_proj, TEAM, axis=0, tiled=True)
    out_part = jnp.einsum(
        "ti,td->id", attn_rows, d_proj_group, preferred_element_type=F32
    ).astype(BF16)
    grad_out = lax.psum_scatter(out_part, "tg", scatter_dimension=0, tiled=True).astype(F32)
    d_kv_parts = [d_kv_sends[0]] + [
        lax.ppermute(d_kv_sends[distance], "tg", next_planes(distance))
        for distance in range(1, planes)
    ]
    d_kv_parts = [part.reshape(rows_group, KV) for part in d_kv_parts]
    head = lax.axis_index("head")
    turns = jnp.stack([heads - 1 - head, head]).astype(jnp.int32)
    d_qkv, theirs = merge_back(turns[:1], d_query, d_kv_parts, own_slab, heads)
    theirs = lax.ppermute(theirs, "head", partner)
    ours = slab_back(turns[1:], d_qkv, own_slab, heads)
    d_qkv, y_back = lax.optimization_barrier((d_qkv, y_back))
    output = (
        valid_float * (hidden_one + jnp.dot(token_table, y_back, preferred_element_type=F32))
    ).astype(BF16)
    grad_in = grad_in_parts(normed_one, d_qkv, extras, planes, in_group)
    grad_planes = lax.all_to_all(grad_in, "tg", split_axis=0, concat_axis=0, tiled=True)
    grad_sum = jnp.sum(grad_planes.astype(F32), axis=0).astype(BF16)
    grad_parts = lax.all_to_all(grad_sum, TEAM, split_axis=0, concat_axis=0, tiled=True)
    ours = (ours.astype(F32) + theirs.astype(F32)).astype(BF16)
    d_normed_one = line_sum(ours.reshape(members, tok_dev, D), member)
    (
        grad_query,
        grad_key,
        grad_value,
        grad_router,
        grad_gain_attn,
        grad_gain_moe,
    ) = finish_grads(grad_parts, by_group, experts)
    scale_one = rms_scale(own_x)
    along_one = gain_one * d_normed_one
    input_grad = (
        d_hidden
        + scale_one * along_one
        - own_x
        * (
            scale_one
            * scale_one
            * scale_one
            * jnp.mean(along_one * own_x, axis=-1, keepdims=True)
        )
    ).astype(BF16)
    return (
        output,
        input_grad,
        grad_query,
        grad_key,
        grad_value,
        grad_out,
        grad_router,
        grad_gain_attn,
        grad_gain_moe,
        grad_gate,
        grad_up,
        grad_down,
    )


def solution(mesh):
    heads = mesh.shape["head"]
    members = HK // heads
    planes = mesh.shape["blk"] // members
    inner = Mesh(mesh.devices.reshape(heads, members, planes), ALL)
    rows = P(ALL, None)
    placed = (
        rows,
        P(),
        rows,
        rows,
        rows,
        rows,
        rows,
        rows,
        P(ALL),
        P(ALL),
        P(BLK, None, "head"),
        P(BLK, None, "head"),
        P(BLK, "head", None),
        rows,
    )
    return jax.shard_map(
        shards,
        mesh=inner,
        in_specs=placed,
        out_specs=(
            rows,
            rows,
            rows,
            rows,
            rows,
            rows,
            rows,
            P(ALL),
            P(ALL),
            P(BLK, None, "head"),
            P(BLK, None, "head"),
            P(BLK, "head", None),
        ),
        check_vma=False,
    )
```

profile of v0, /device:TPU:0, one launch (start us, length us, event | category | flops | bytes accessed | tf_op | source)
XLA Modules:
  0.0 478.7 jit_solution(17038087123997231487)
XLA Ops:
  8.8 1.7 concatenate.13
  13.8 6.4 %all-to-all-start.1 = ((bf16[8,48,384]{2,1,0:T(8,128)(2,1)}), bf16[8,48,384]{2,1,0:T(8,128)(2,1)S(1)}, u32[]{:S(2)}, u32[]{:S(2)}) async-start(bf16[8,48,384]{2,1,0:T(8,128)(2,1)} %bitcast.8.slab_ref), calls=%async_computation.1 | async-start | bytes 589824 | tf_op jit(solution)/shard_map/all_to_all | solution.py:758
  22.1 10.0 %all-to-all-done.1 = bf16[8,48,384]{2,1,0:T(8,128)(2,1)S(1)} async-done(((bf16[8,48,384]{2,1,0:T(8,128)(2,1)}), bf16[8,48,384]{2,1,0:T(8,128)(2,1)S(1)}, u32[]{:S(2)}, u32[]{:S(2)}) %all-to-all-start.1) | async-done | bytes 294944 | tf_op jit(solution)/shard_map/all_to_all | solution.py:758
  33.3 4.0 all-to-all-start.2
  41.4 16.3 %all-to-all-done.2.refs_14_ = bf16[4,8,48,384]{3,2,1,0:T(8,128)(2,1)S(1)} async-done(((bf16[4,8,48,384]{3,2,1,0:T(8,128)(2,1)}), bf16[4,8,48,384]{3,2,1,0:T(8,128)(2,1)S(1)}, u32[]{:S(2)}, u32[]{:S(2)}) %all-to-all-start.2) | async-done | bytes 1179680 | tf_op jit(solution)/shard_map/all_to_all | solution.py:761
  57.7 3.7 all-to-all-start
  61.4 3.8 collective-permute-start
  66.5 36.1 %collective-permute-done.refs_2_ = bf16[128,1536]{1,0:T(8,128)(2,1)S(1)} collective-permute-done((bf16[128,1536]{1,0:T(8,128)(2,1)S(1)}, bf16[128,1536]{1,0:T(8,128)(2,1)S(1)}, u32[]{:S(2)}, u32[]{:S(2)}) %collective-permute-start) | collective-permute-done | bytes 393248 | tf_op jit(solution)/shard_map/ppermute | solution.py:333
  102.5 2.1 collective-permute-done.1.refs_4_
  106.6 17.9 %collective-permute-done.3.refs_5_ = bf16[128,1536]{1,0:T(8,128)(2,1)S(1)} collective-permute-done((bf16[128,1536]{1,0:T(8,128)(2,1)S(1)}, bf16[128,1536]{1,0:T(8,128)(2,1)S(1)}, u32[]{:S(2)}, u32[]{:S(2)}) %collective-permute-start.3) | collective-permute-done | bytes 393248 | tf_op jit(solution)/shard_map/ppermute | solution.py:334
  127.6 8.4 %collective-permute-done.5.refs_6_ = bf16[128,1536]{1,0:T(8,128)(2,1)S(1)} collective-permute-done((bf16[128,1536]{1,0:T(8,128)(2,1)S(1)}, bf16[128,1536]{1,0:T(8,128)(2,1)S(1)}, u32[]{:S(2)}, u32[]{:S(2)}) %collective-permute-start.5) | collective-permute-done | bytes 393248 | tf_op jit(solution)/shard_map/ppermute | solution.py:334
  138.9 7.1 %project.1 = (bf16[1024,1536]{1,0:T(8,128)(2,1)S(1)}, bf16[1024,192]{1,0:T(8,128)(2,1)S(1)}, bf16[1024,128]{1,0:T(8,128)(2,1)S(1)}, bf16[1536,384]{1,0:T(8,128)(2,1)S(1)}, f32[1,1536]{1,0:T(1,128)S(1)}) custom-call(s32[2]{0:T(128)S(1)} %pad_add_fusion.place_ref, bf16[128,1536]{1,0:T(8,128)(2,1)S(1)} %collective-permute-done.4.refs_0_, ...), custom_call_target="tpu_custom_call" | custom-call | tf_op jit(solution)/shard_map/project/pallas_call | solution.py:305
  147.0 1.8 copy-done.15
  150.3 2.5 collective-permute-start.14
  154.2 5.2 %collective-permute-done.13.refs_1_ = bf16[8,128,128]{2,1,0:T(8,128)(2,1)S(1)} collective-permute-done((bf16[8,128,128]{2,1,0:T(8,128)(2,1)S(1)}, bf16[8,128,128]{2,1,0:T(8,128)(2,1)S(1)}, u32[]{:S(2)}, u32[]{:S(2)}) %collective-permute-start.13) | collective-permute-done | bytes 262176 | tf_op jit(solution)/shard_map/ppermute | solution.py:834
  159.4 5.0 %collective-permute-done.14.refs_2_ = bf16[8,128,128]{2,1,0:T(8,128)(2,1)S(1)} collective-permute-done((bf16[8,128,128]{2,1,0:T(8,128)(2,1)S(1)}, bf16[8,128,128]{2,1,0:T(8,128)(2,1)S(1)}, u32[]{:S(2)}, u32[]{:S(2)}) %collective-permute-start.14) | collective-permute-done | bytes 262176 | tf_op jit(solution)/shard_map/ppermute | solution.py:834
  164.8 11.3 %attend.1 = (bf16[1024,192]{1,0:T(8,128)(2,1)S(1)}, f32[8,1,384]{2,1,0:T(1,128)S(1)}) custom-call(s32[12]{0:T(128)S(1)} %copy-done.41, s32[1]{0:T(128)} %bitcast.5.meta_ref, bf16[1024,192]{1,0:T(8,128)(2,1)S(1)} %get-tuple-element.65.q_ref, bf16[8,128,128]{2,1,0:T(8,128)(2,1)S(1)} %bitcast.112, bf16[8,128,128]{2,1,0:T(8,128)(2,1)S(1)} %collective-permute-done.13.refs_1_, ...), custom_call_target="tpu_custom_call" | custom-call | tf_op jit(solution)/shard_map/attend/pallas_call | solution.py:230
  180.7 3.5 all-to-all-start.3
  184.2 11.9 %all-to-all-done.3 = bf16[8,128,192]{1,2,0:T(8,128)(2,1)S(1)} async-done(((bf16[8,128,192]{1,2,0:T(8,128)(2,1)}), bf16[8,128,192]{1,2,0:T(8,128)(2,1)S(1)}, u32[]{:S(2)}, u32[]{:S(2)}) %all-to-all-start.3) | async-done | bytes 393248 | tf_op jit(solution)/shard_map/all_to_all | solution.py:841
  196.1 3.2 multiply_reduce_fusion.1
  203.7 35.7 %all_to_all.78 = bf16[16,24,1664]{2,1,0:T(8,128)(2,1)S(1)} all-to-all(bf16[16,24,1664]{2,1,0:T(8,128)(2,1)S(1)} %bitcast.123), channel_id=1, replica_groups=mesh['head'=2,'hg'=4,'tg'=4] {'hg','tg'}, dimensions={0} | all-to-all | bytes 2555904 | tf_op jit(solution)/shard_map/all_to_all | solution.py:809
  239.9 4.2 collective-permute-done.17.d_other_ref
  244.1 2.3 copy-done.23
  246.4 10.1 %expert.1 = (bf16[768,1664]{1,0:T(8,128)(2,1)S(1)}, bf16[768,512]{1,0:T(8,128)(2,1)S(1)}, bf16[768,512]{1,0:T(8,128)(2,1)S(1)}, bf16[768,512]{1,0:T(8,128)(2,1)S(1)}) custom-call(s32[1]{0:T(128)} %bitcast.15.expert_ref, bf16[384,1664]{1,0:T(8,128)(2,1)S(1)} %bitcast.98, bf16[384,1664]{1,0:T(8,128)(2,1)S(1)} %collective-permute-done.16.x_other_ref, ...), custom_call_target="tpu_custom_call" | custom-call | tf_op jit(solution)/shard_map/expert/pallas_call | solution.py:485
  256.9 2.9 collective-permute-done.18.other_ref
  261.7 4.6 all-to-all-start.5
  266.3 3.0 fusion.39
  269.3 2.2 copy-done.49
  272.8 22.5 %all-to-all-done.5 = bf16[16,24,1664]{2,1,0:T(8,128)(2,1)} async-done(((bf16[16,24,1664]{2,1,0:T(8,128)(2,1)}), bf16[16,24,1664]{2,1,0:T(8,128)(2,1)}, u32[]{:S(2)}, u32[]{:S(2)}) %all-to-all-start.5) | async-done | bytes 1277984 | tf_op jit(solution)/shard_map/all_to_all | solution.py:809
  295.3 1.8 fusion.23
  300.1 2.6 copy-done
  302.7 2.0 attn_back.1
  305.5 1.9 copy.78
  307.4 5.6 %all-to-all-start.6 = ((bf16[128,8,192]{0,2,1:T(8,128)(2,1)}), bf16[128,8,192]{0,2,1:T(8,128)(2,1)S(1)}, u32[]{:S(2)}, u32[]{:S(2)}) async-start(bf16[128,8,192]{0,2,1:T(8,128)(2,1)} %bitcast.127), calls=%async_computation.6 | async-start | bytes 786432 | tf_op jit(solution)/shard_map/all_to_all | solution.py:906
  313.1 3.3 fusion.7
  316.5 8.6 %all-to-all-done.6 = bf16[128,8,192]{0,2,1:T(8,128)(2,1)S(1)} async-done(((bf16[128,8,192]{0,2,1:T(8,128)(2,1)}), bf16[128,8,192]{0,2,1:T(8,128)(2,1)S(1)}, u32[]{:S(2)}, u32[]{:S(2)}) %all-to-all-start.6) | async-done | bytes 393248 | tf_op jit(solution)/shard_map/all_to_all | solution.py:906
  331.8 14.8 %attend_back.1 = (bf16[1024,192]{1,0:T(8,128)(2,1)S(1)}, bf16[8,128,128]{2,1,0:T(8,128)(2,1)S(1)}, bf16[8,128,128]{2,1,0:T(8,128)(2,1)S(1)}, bf16[8,128,128]{2,1,0:T(8,128)(2,1)S(1)}, bf16[8,128,128]{2,1,0:T(8,128)(2,1)S(1)}) custom-call(s32[12]{0:T(128)S(1)} %copy-done.41, s32[1]{0:T(128)} %bitcast.5.meta_ref, bf16[1024,192]{1,0:T(8,128)(2,1)S(1)} %copy-done.21, ...), custom_call_target="tpu_custom_call" | custom-call | tf_op jit(solution)/shard_map/attend_back/pallas_call | solution.py:249
  350.3 4.0 collective-permute-start.21
  354.4 2.8 collective-permute-start.22
  357.2 3.5 collective-permute-done.20
  360.7 5.7 %collective-permute-done.21 = bf16[8,128,128]{2,1,0:T(8,128)(2,1)S(1)} collective-permute-done((bf16[8,128,128]{2,1,0:T(8,128)(2,1)}, bf16[8,128,128]{2,1,0:T(8,128)(2,1)S(1)}, u32[]{:S(2)}, u32[]{:S(2)}) %collective-permute-start.21) | collective-permute-done | bytes 262176 | tf_op jit(solution)/shard_map/ppermute | solution.py:917
  366.4 1.9 collective-permute-done.22
  371.5 3.7 merge_back.1
  376.2 4.4 all-to-all-start.7
  384.2 1.8 add_convert_fusion
  388.0 4.5 collective-permute-start.24
  399.9 9.1 %expert_grads.1 = (f32[1,1536,512]{2,1,0:T(8,128)}, f32[1,1536,512]{2,1,0:T(8,128)}, f32[1,512,1536]{2,1,0:T(8,128)}) custom-call(bf16[384,1664]{1,0:T(8,128)(2,1)S(1)} %bitcast.99, bf16[384,1664]{1,0:T(8,128)(2,1)S(1)} %copy-done.3, bf16[384,1536]{1,0:T(8,128)(2,1)S(1)} %bitcast.102, bf16[384,1536]{1,0:T(8,128)(2,1)S(1)} %copy-done.6, ...), custom_call_target="tpu_custom_call" | custom-call | tf_op jit(solution)/shard_map/expert_grads/pallas_call | solution.py:555
  409.5 2.0 collective-permute-done.24
  411.6 2.2 fusion.13
  413.8 5.2 %collective-permute-start.26 = (bf16[128,1536]{1,0:T(8,128)(2,1)}, bf16[128,1536]{1,0:T(8,128)(2,1)}, u32[]{:S(2)}, u32[]{:S(2)}) collective-permute-start(bf16[128,1536]{1,0:T(8,128)(2,1)} %get-tuple-element.165), channel_id=1, source_target_pairs={{0,4},{4,8},{1,5},{5,9},{2,6},{6,10},{3,7},{7,11},{16,20},{20,24},... | collective-permute-start | bytes 1179656 | tf_op jit(solution)/shard_map/ppermute | solution.py:704
  421.3 1.9 copy-done.16
  423.2 3.5 grad_in.1
  426.7 4.4 all-to-all-start.8
  431.2 2.2 fusion.12
  433.4 5.3 %collective-permute-start.28 = (bf16[128,1536]{1,0:T(8,128)(2,1)}, bf16[128,1536]{1,0:T(8,128)(2,1)}, u32[]{:S(2)}, u32[]{:S(2)}) collective-permute-start(bf16[128,1536]{1,0:T(8,128)(2,1)} %get-tuple-element.163), channel_id=1, source_target_pairs={{0,4},{4,8},{8,12},{1,5},{5,9},{9,13},{2,6},{6,10},{10,14},{3,7},{... | collective-permute-start | bytes 1179656 | tf_op jit(solution)/shard_map/ppermute | solution.py:704
  440.1 3.5 convolution_convert_fusion.2
  443.6 2.5 fusion.6
  446.1 4.4 collective-permute-done.29
  452.1 2.2 reduce_sum.85
  454.3 3.4 all-to-all-start.9
  457.8 2.2 fusion.11
  459.9 7.8 %all-to-all-done.9.parts_ref = bf16[8,48,384]{2,1,0:T(8,128)(2,1)S(1)} async-done(((bf16[8,48,384]{2,1,0:T(8,128)(2,1)}), bf16[8,48,384]{2,1,0:T(8,128)(2,1)S(1)}, u32[]{:S(2)}, u32[]{:S(2)}) %all-to-all-start.9) | async-done | bytes 294944 | tf_op jit(solution)/shard_map/all_to_all | solution.py:933
  467.7 2.2 finish_grads.1
  470.6 1.6 convert_element_type.190
  (247 shorter events, 76.2 us)
Async XLA Ops:
  7.2 5.4 %copy-start.63 = (bf16[48,512]{1,0:T(8,128)(2,1)S(1)}, bf16[48,512]{1,0:T(8,128)(2,1)}, u32[]{:S(2)}) copy-start(bf16[48,512]{1,0:T(8,128)(2,1)} %param.19) | copy-start | bytes 147460
  7.2 5.6 %copy-start.65 = (bf16[48]{0:T(256)(128)(2,1)S(1)}, bf16[48]{0:T(256)(128)(2,1)}, u32[]{:S(2)}) copy-start(bf16[48]{0:T(256)(128)(2,1)} %param.22) | copy-start | bytes 292
  7.2 188.9 %all-gather.3.cloned.1.call-start = ((), (), s32[]{:S(2)}) async-start(), calls=%async_computation.11 | async-start | bytes 5271552 | tf_op jit(solution)/shard_map/all_gather | solution.py:778
  10.5 9.7 %copy-start.64 = (s32[128,2]{0,1:T(2,128)S(1)}, s32[128,2]{0,1:T(2,128)}, u32[]{:S(2)}) copy-start(s32[128,2]{0,1:T(2,128)} %param.16) | copy-start | bytes 3076
  10.5 9.8 %copy-start.41 = (s32[12]{0:T(128)S(1)}, s32[12]{0:T(128)}, u32[]{:S(2)}) copy-start(s32[12]{0:T(128)} %lengths_ref.3) | copy-start | bytes 148
  13.8 18.3 %all-to-all-start.1 = ((bf16[8,48,384]{2,1,0:T(8,128)(2,1)}), bf16[8,48,384]{2,1,0:T(8,128)(2,1)S(1)}, u32[]{:S(2)}, u32[]{:S(2)}) async-start(bf16[8,48,384]{2,1,0:T(8,128)(2,1)} %bitcast.8.slab_ref), calls=%async_computation.1 | async-start | bytes 589824 | tf_op jit(solution)/shard_map/all_to_all | solution.py:758
  33.3 6.5 %copy-start.58 = (bf16[128,1536]{1,0:T(8,128)(2,1)S(1)}, bf16[128,1536]{1,0:T(8,128)(2,1)}, u32[]{:S(2)}) copy-start(bf16[128,1536]{1,0:T(8,128)(2,1)} %param.27) | copy-start | bytes 1179652
  33.3 24.4 %all-to-all-start.2 = ((bf16[4,8,48,384]{3,2,1,0:T(8,128)(2,1)}), bf16[4,8,48,384]{3,2,1,0:T(8,128)(2,1)S(1)}, u32[]{:S(2)}, u32[]{:S(2)}) async-start(bf16[4,8,48,384]{3,2,1,0:T(8,128)(2,1)} %broadcast_in_dim.59), calls=%async_computation.2 | async-start | bytes 2359296 | tf_op jit(solution)/shard_map/all_to_all | solution.py:761
  41.4 20.0 %copy-start.11 = (bf16[128,1536]{1,0:T(8,128)(2,1)S(1)}, bf16[128,1536]{1,0:T(8,128)(2,1)}, u32[]{:S(2)}) copy-start(bf16[128,1536]{1,0:T(8,128)(2,1)} %refs_3_.1) | copy-start | bytes 1179652
  57.7 122.1 %all-to-all-start = ((bf16[16,24,1536]{2,1,0:T(8,128)(2,1)}), bf16[16,24,1536]{2,1,0:T(8,128)(2,1)S(1)}, u32[]{:S(2)}, u32[]{:S(2)}) async-start(bf16[16,24,1536]{2,1,0:T(8,128)(2,1)} %bitcast.124), calls=%async_computation | async-start | bytes 2359296 | tf_op jit(solution)/shard_map/all_to_all | solution.py:809
  61.4 41.1 %collective-permute-start = (bf16[128,1536]{1,0:T(8,128)(2,1)S(1)}, bf16[128,1536]{1,0:T(8,128)(2,1)S(1)}, u32[]{:S(2)}, u32[]{:S(2)}) collective-permute-start(bf16[128,1536]{1,0:T(8,128)(2,1)S(1)} %copy-done.11), channel_id=1, source_target_pairs={{0,4},{4,8},{8,12},{1,5},{5,9},{9,13},{2,6},{6,10},{10,14},{3,7},{... | collective-permute-start | bytes 1179656 | tf_op jit(solution)/shard_map/ppermute | solution.py:333
  65.2 39.5 %collective-permute-start.1 = (bf16[128,1536]{1,0:T(8,128)(2,1)S(1)}, bf16[128,1536]{1,0:T(8,128)(2,1)S(1)}, u32[]{:S(2)}, u32[]{:S(2)}) collective-permute-start(bf16[128,1536]{1,0:T(8,128)(2,1)S(1)} %copy-done.11), channel_id=1, source_target_pairs={{12,8},{8,4},{4,0},{13,9},{9,5},{5,1},{14,10},{10,6},{6,2},{15,11}... | collective-permute-start | bytes 1179656 | tf_op jit(solution)/shard_map/ppermute | solution.py:334
  104.6 2.0 collective-permute-start.2
  105.3 19.2 %collective-permute-start.3 = (bf16[128,1536]{1,0:T(8,128)(2,1)S(1)}, bf16[128,1536]{1,0:T(8,128)(2,1)S(1)}, u32[]{:S(2)}, u32[]{:S(2)}) collective-permute-start(bf16[128,1536]{1,0:T(8,128)(2,1)S(1)} %collective-permute-done.1.refs_4_), channel_id=1, source_target_pairs={{8,4},{4,0},{9,5},{5,1},{10,6},{6,2},{11,7},{7,3},{24,20},{20,16},... | collective-permute-start | bytes 1179656 | tf_op jit(solution)/shard_map/ppermute | solution.py:334
  124.5 2.6 collective-permute-start.4
  125.2 10.8 %collective-permute-start.5 = (bf16[128,1536]{1,0:T(8,128)(2,1)S(1)}, bf16[128,1536]{1,0:T(8,128)(2,1)S(1)}, u32[]{:S(2)}, u32[]{:S(2)}) collective-permute-start(bf16[128,1536]{1,0:T(8,128)(2,1)S(1)} %collective-permute-done.3.refs_5_), channel_id=1, source_target_pairs={{4,0},{5,1},{6,2},{7,3},{20,16},{21,17},{22,18},{23,19}} | collective-permute-start | bytes 1179656 | tf_op jit(solution)/shard_map/ppermute | solution.py:334
  126.5 9.5 %collective-permute-start.9 = (bf16[128,1536]{1,0:T(8,128)(2,1)S(1)}, bf16[128,1536]{1,0:T(8,128)(2,1)S(1)}, u32[]{:S(2)}, u32[]{:S(2)}) collective-permute-start(bf16[128,1536]{1,0:T(8,128)(2,1)S(1)} %copy-done.11), channel_id=1, source_target_pairs={{0,16},{16,0},{1,17},{17,1},{2,18},{18,2},{3,19},{19,3},{4,20},{20... | collective-permute-start | bytes 1179656 | tf_op jit(solution)/shard_map/ppermute | solution.py:330
  126.6 9.9 %collective-permute-start.8 = (bf16[128,1536]{1,0:T(8,128)(2,1)S(1)}, bf16[128,1536]{1,0:T(8,128)(2,1)S(1)}, u32[]{:S(2)}, u32[]{:S(2)}) collective-permute-start(bf16[128,1536]{1,0:T(8,128)(2,1)S(1)} %collective-permute-done.refs_2_), channel_id=1, source_target_pairs={{0,16},{16,0},{1,17},{17,1},{2,18},{18,2},{3,19},{19,3},{4,20},{20... | collective-permute-start | bytes 1179656 | tf_op jit(solution)/shard_map/ppermute | solution.py:337
  127.1 9.6 %collective-permute-start.10 = (bf16[128,1536]{1,0:T(8,128)(2,1)S(1)}, bf16[128,1536]{1,0:T(8,128)(2,1)S(1)}, u32[]{:S(2)}, u32[]{:S(2)}) collective-permute-start(bf16[128,1536]{1,0:T(8,128)(2,1)S(1)} %collective-permute-done.1.refs_4_), channel_id=1, source_target_pairs={{0,16},{16,0},{1,17},{17,1},{2,18},{18,2},{3,19},{19,3},{4,20},{20... | collective-permute-start | bytes 1179656 | tf_op jit(solution)/shard_map/ppermute | solution.py:338
  127.2 9.5 %collective-permute-start.7 = (bf16[128,1536]{1,0:T(8,128)(2,1)S(1)}, bf16[128,1536]{1,0:T(8,128)(2,1)S(1)}, u32[]{:S(2)}, u32[]{:S(2)}) collective-permute-start(bf16[128,1536]{1,0:T(8,128)(2,1)S(1)} %collective-permute-done.2.refs_1_), channel_id=1, source_target_pairs={{0,16},{16,0},{1,17},{17,1},{2,18},{18,2},{3,19},{19,3},{4,20},{20... | collective-permute-start | bytes 1179656 | tf_op jit(solution)/shard_map/ppermute | solution.py:337
  136.0 1.7 collective-permute-start.11
  136.0 2.3 collective-permute-start.6
  136.5 2.3 collective-permute-start.12
  148.8 10.6 %collective-permute-start.13 = (bf16[8,128,128]{2,1,0:T(8,128)(2,1)S(1)}, bf16[8,128,128]{2,1,0:T(8,128)(2,1)S(1)}, u32[]{:S(2)}, u32[]{:S(2)}) collective-permute-start(bf16[8,128,128]{2,1,0:T(8,128)(2,1)S(1)} %bitcast.109), channel_id=1, source_target_pairs={{0,1},{1,2},{2,3},{3,0},{4,5},{5,6},{6,7},{7,4},{8,9},{9,10},{10,1... | collective-permute-start | bytes 786440 | tf_op jit(solution)/shard_map/ppermute | solution.py:834
  150.3 14.2 %collective-permute-start.14 = (bf16[8,128,128]{2,1,0:T(8,128)(2,1)S(1)}, bf16[8,128,128]{2,1,0:T(8,128)(2,1)S(1)}, u32[]{:S(2)}, u32[]{:S(2)}) collective-permute-start(bf16[8,128,128]{2,1,0:T(8,128)(2,1)S(1)} %bitcast.110), channel_id=1, source_target_pairs={{0,2},{1,3},{2,0},{3,1},{4,6},{5,7},{6,4},{7,5},{8,10},{9,11},{10,... | collective-permute-start | bytes 786440 | tf_op jit(solution)/shard_map/ppermute | solution.py:834
  152.8 12.0 %collective-permute-start.15 = (bf16[8,128,128]{2,1,0:T(8,128)(2,1)S(1)}, bf16[8,128,128]{2,1,0:T(8,128)(2,1)S(1)}, u32[]{:S(2)}, u32[]{:S(2)}) collective-permute-start(bf16[8,128,128]{2,1,0:T(8,128)(2,1)S(1)} %bitcast.111), channel_id=1, source_target_pairs={{0,3},{1,0},{2,1},{3,2},{4,7},{5,4},{6,5},{7,6},{8,11},{9,8},{10,9... | collective-permute-start | bytes 786440 | tf_op jit(solution)/shard_map/ppermute | solution.py:834
  180.7 15.4 %all-to-all-start.3 = ((bf16[8,128,192]{1,2,0:T(8,128)(2,1)}), bf16[8,128,192]{1,2,0:T(8,128)(2,1)S(1)}, u32[]{:S(2)}, u32[]{:S(2)}) async-start(bf16[8,128,192]{1,2,0:T(8,128)(2,1)} %copy.74), calls=%async_computation.3 | async-start | bytes 786432 | tf_op jit(solution)/shard_map/all_to_all | solution.py:841
  203.0 41.1 %copy-start.22 = (bf16[1,1536,512]{2,1,0:T(8,128)(2,1)S(1)}, bf16[1,1536,512]{2,1,0:T(8,128)(2,1)}, u32[]{:S(2)}) copy-start(bf16[1,1536,512]{2,1,0:T(8,128)(2,1)} %param.24) | copy-start | bytes 4718596
  203.7 40.4 %copy-start.1 = (bf16[1,512,1536]{2,1,0:T(8,128)(2,1)S(1)}, bf16[1,512,1536]{2,1,0:T(8,128)(2,1)}, u32[]{:S(2)}) copy-start(bf16[1,512,1536]{2,1,0:T(8,128)(2,1)} %param.26) | copy-start | bytes 4718596
  239.4 4.7 collective-permute-start.16
  239.4 4.7 collective-permute-start.17
  244.1 12.4 %copy-start.5 = (bf16[384,1536]{1,0:T(8,128)(2,1)}, bf16[384,1536]{1,0:T(8,128)(2,1)S(1)}, u32[]{:S(2)}) copy-start(bf16[384,1536]{1,0:T(8,128)(2,1)S(1)} %collective-permute-done.17.d_other_ref) | copy-start | bytes 3538948
  244.1 12.4 %copy-start.2 = (bf16[384,1664]{1,0:T(8,128)(2,1)}, bf16[384,1664]{1,0:T(8,128)(2,1)S(1)}, u32[]{:S(2)}) copy-start(bf16[384,1664]{1,0:T(8,128)(2,1)S(1)} %collective-permute-done.16.x_other_ref) | copy-start | bytes 3833860
  256.5 4.1 copy-start.13
  256.6 4.1 copy-start.33
  256.6 4.1 copy-start.35
  256.7 3.1 collective-permute-start.18
  261.7 33.6 %all-to-all-start.5 = ((bf16[16,24,1664]{2,1,0:T(8,128)(2,1)}), bf16[16,24,1664]{2,1,0:T(8,128)(2,1)}, u32[]{:S(2)}, u32[]{:S(2)}) async-start(bf16[16,24,1664]{2,1,0:T(8,128)(2,1)} %bitcast.104), calls=%async_computation.5 | async-start | bytes 2555904 | tf_op jit(solution)/shard_map/all_to_all | solution.py:809
  272.7 40.4 %collective-permute-start.19 = (bf16[384,1536]{1,0:T(8,128)(2,1)}, bf16[384,1536]{1,0:T(8,128)(2,1)}, u32[]{:S(2)}, u32[]{:S(2)}) collective-permute-start(bf16[384,1536]{1,0:T(8,128)(2,1)} %slice.106), channel_id=1, source_target_pairs={{0,16},{16,0},{1,17},{17,1},{2,18},{18,2},{3,19},{19,3},{4,20},{20... | collective-permute-start | bytes 3538952 | tf_op jit(solution)/shard_map/ppermute | solution.py:867
  300.1 4.6 copy-start.10
  307.4 17.6 %all-to-all-start.6 = ((bf16[128,8,192]{0,2,1:T(8,128)(2,1)}), bf16[128,8,192]{0,2,1:T(8,128)(2,1)S(1)}, u32[]{:S(2)}, u32[]{:S(2)}) async-start(bf16[128,8,192]{0,2,1:T(8,128)(2,1)} %bitcast.127), calls=%async_computation.6 | async-start | bytes 786432 | tf_op jit(solution)/shard_map/all_to_all | solution.py:906
  313.1 127.0 %all-gather.5.cloned.1.call-start = ((), (), s32[]{:S(2)}) async-start(), calls=%async_computation.12 | async-start | bytes 3538944 | tf_op jit(solution)/shard_map/all_gather | solution.py:911
  350.3 10.4 %collective-permute-start.20 = (bf16[8,128,128]{2,1,0:T(8,128)(2,1)}, bf16[8,128,128]{2,1,0:T(8,128)(2,1)S(1)}, u32[]{:S(2)}, u32[]{:S(2)}) collective-permute-start(bf16[8,128,128]{2,1,0:T(8,128)(2,1)} %copy-done.44), channel_id=1, source_target_pairs={{0,1},{1,2},{2,3},{3,0},{4,5},{5,6},{6,7},{7,4},{8,9},{9,10},{10,1... | collective-permute-start | bytes 786440 | tf_op jit(solution)/shard_map/ppermute | solution.py:917
  350.3 16.0 %collective-permute-start.21 = (bf16[8,128,128]{2,1,0:T(8,128)(2,1)}, bf16[8,128,128]{2,1,0:T(8,128)(2,1)S(1)}, u32[]{:S(2)}, u32[]{:S(2)}) collective-permute-start(bf16[8,128,128]{2,1,0:T(8,128)(2,1)} %copy-done.43), channel_id=1, source_target_pairs={{0,2},{1,3},{2,0},{3,1},{4,6},{5,7},{6,4},{7,5},{8,10},{9,11},{10,... | collective-permute-start | bytes 786440 | tf_op jit(solution)/shard_map/ppermute | solution.py:917
  354.4 13.9 %collective-permute-start.22 = (bf16[8,128,128]{2,1,0:T(8,128)(2,1)}, bf16[8,128,128]{2,1,0:T(8,128)(2,1)}, u32[]{:S(2)}, u32[]{:S(2)}) collective-permute-start(bf16[8,128,128]{2,1,0:T(8,128)(2,1)} %copy-done.42), channel_id=1, source_target_pairs={{0,3},{1,0},{2,1},{3,2},{4,7},{5,4},{6,5},{7,6},{8,11},{9,8},{10,9... | collective-permute-start | bytes 786440 | tf_op jit(solution)/shard_map/ppermute | solution.py:917
  376.2 8.0 %collective-permute-start.23 = (bf16[512,1536]{1,0:T(8,128)(2,1)}, bf16[512,1536]{1,0:T(8,128)(2,1)}, u32[]{:S(2)}, u32[]{:S(2)}) collective-permute-start(bf16[512,1536]{1,0:T(8,128)(2,1)} %get-tuple-element.85), channel_id=1, source_target_pairs={{0,16},{16,0},{1,17},{17,1},{2,18},{18,2},{3,19},{19,3},{4,20},{20... | collective-permute-start | bytes 4718600 | tf_op jit(solution)/shard_map/ppermute | solution.py:924
  376.2 45.1 %all-to-all-start.7 = ((bf16[16,24,1536]{2,1,0:T(8,128)(2,1)}), bf16[16,24,1536]{2,1,0:T(8,128)(2,1)}, u32[]{:S(2)}, u32[]{:S(2)}) async-start(bf16[16,24,1536]{2,1,0:T(8,128)(2,1)} %bitcast.125), calls=%async_computation.7 | async-start | bytes 2359296 | tf_op jit(solution)/shard_map/all_to_all | solution.py:809
  388.0 23.6 %collective-permute-start.24 = (bf16[128,1536]{1,0:T(8,128)(2,1)}, bf16[128,1536]{1,0:T(8,128)(2,1)}, u32[]{:S(2)}, u32[]{:S(2)}) collective-permute-start(bf16[128,1536]{1,0:T(8,128)(2,1)} %get-tuple-element.167), channel_id=1, source_target_pairs={{0,4},{1,5},{2,6},{3,7},{16,20},{17,21},{18,22},{19,23}} | collective-permute-start | bytes 1179656 | tf_op jit(solution)/shard_map/ppermute | solution.py:704
  392.5 19.1 %collective-permute-start.25 = (bf16[128,1536]{1,0:T(8,128)(2,1)S(1)}, bf16[128,1536]{1,0:T(8,128)(2,1)}, u32[]{:S(2)}, u32[]{:S(2)}) collective-permute-start(bf16[128,1536]{1,0:T(8,128)(2,1)S(1)} %get-tuple-element.166), channel_id=1, source_target_pairs={{12,8},{13,9},{14,10},{15,11},{28,24},{29,25},{30,26},{31,27}} | collective-permute-start | bytes 1179656 | tf_op jit(solution)/shard_map/ppermute | solution.py:705
  399.9 9.1 %copy-start.47 = (f32[128,1536]{1,0:T(8,128)S(1)}, f32[128,1536]{1,0:T(8,128)}, u32[]{:S(2)}) copy-start(f32[128,1536]{1,0:T(8,128)} %copy-done.45) | copy-start | bytes 2359300
  399.9 9.1 %copy-start.54 = (f32[128,1536]{1,0:T(8,128)S(1)}, f32[128,1536]{1,0:T(8,128)}, u32[]{:S(2)}) copy-start(f32[128,1536]{1,0:T(8,128)} %copy-done.53) | copy-start | bytes 2359300
  409.5 10.9 %copy-start.56 = (bf16[128,1536]{1,0:T(8,128)(2,1)S(1)}, bf16[128,1536]{1,0:T(8,128)(2,1)}, u32[]{:S(2)}) copy-start(bf16[128,1536]{1,0:T(8,128)(2,1)} %copy-done.55) | copy-start | bytes 1179652
  409.5 10.9 %copy-start.62 = (bf16[128,16]{1,0:T(8,128)(2,1)S(1)}, bf16[128,16]{1,0:T(8,128)(2,1)}, u32[]{:S(2)}) copy-start(bf16[128,16]{1,0:T(8,128)(2,1)} %copy-done.61) | copy-start | bytes 12292
  413.8 17.4 %collective-permute-start.26 = (bf16[128,1536]{1,0:T(8,128)(2,1)}, bf16[128,1536]{1,0:T(8,128)(2,1)}, u32[]{:S(2)}, u32[]{:S(2)}) collective-permute-start(bf16[128,1536]{1,0:T(8,128)(2,1)} %get-tuple-element.165), channel_id=1, source_target_pairs={{0,4},{4,8},{1,5},{5,9},{2,6},{6,10},{3,7},{7,11},{16,20},{20,24},... | collective-permute-start | bytes 1179656 | tf_op jit(solution)/shard_map/ppermute | solution.py:704
  418.9 12.3 %collective-permute-start.27 = (bf16[128,1536]{1,0:T(8,128)(2,1)}, bf16[128,1536]{1,0:T(8,128)(2,1)}, u32[]{:S(2)}, u32[]{:S(2)}) collective-permute-start(bf16[128,1536]{1,0:T(8,128)(2,1)} %get-tuple-element.164), channel_id=1, source_target_pairs={{12,8},{8,4},{13,9},{9,5},{14,10},{10,6},{15,11},{11,7},{28,24},{2... | collective-permute-start | bytes 1179656 | tf_op jit(solution)/shard_map/ppermute | solution.py:705
  426.7 4.5 copy-start.52
  426.7 25.4 %all-to-all-start.8 = ((bf16[4,8,48,384]{3,2,1,0:T(8,128)(2,1)}), bf16[4,8,48,384]{3,2,1,0:T(8,128)(2,1)}, u32[]{:S(2)}, u32[]{:S(2)}) async-start(bf16[4,8,48,384]{3,2,1,0:T(8,128)(2,1)} %grad_in.1), calls=%async_computation.8 | async-start | bytes 2359296 | tf_op jit(solution)/shard_map/all_to_all | solution.py:931
  431.1 39.4 %reduce-scatter.2.cloned.1.call-start = ((), (), s32[]{:S(2)}) async-start(), calls=%async_computation.13 | async-start | bytes 737280 | tf_op jit(solution)/shard_map/reduce_scatter | solution.py:915
  433.4 12.8 %collective-permute-start.28 = (bf16[128,1536]{1,0:T(8,128)(2,1)}, bf16[128,1536]{1,0:T(8,128)(2,1)}, u32[]{:S(2)}, u32[]{:S(2)}) collective-permute-start(bf16[128,1536]{1,0:T(8,128)(2,1)} %get-tuple-element.163), channel_id=1, source_target_pairs={{0,4},{4,8},{8,12},{1,5},{5,9},{9,13},{2,6},{6,10},{10,14},{3,7},{... | collective-permute-start | bytes 1179656 | tf_op jit(solution)/shard_map/ppermute | solution.py:704
  438.6 5.0 %copy-start.48 = (f32[128,1536]{1,0:T(8,128)S(1)}, f32[128,1536]{1,0:T(8,128)}, u32[]{:S(2)}) copy-start(f32[128,1536]{1,0:T(8,128)} %copy-done.45) | copy-start | bytes 2359300
  438.6 11.9 %collective-permute-start.29 = (bf16[128,1536]{1,0:T(8,128)(2,1)}, bf16[128,1536]{1,0:T(8,128)(2,1)}, u32[]{:S(2)}, u32[]{:S(2)}) collective-permute-start(bf16[128,1536]{1,0:T(8,128)(2,1)} %get-tuple-element.162), channel_id=1, source_target_pairs={{12,8},{8,4},{4,0},{13,9},{9,5},{5,1},{14,10},{10,6},{6,2},{15,11}... | collective-permute-start | bytes 1179656 | tf_op jit(solution)/shard_map/ppermute | solution.py:705
  443.6 7.0 %copy-start.12 = (bf16[128,1536]{1,0:T(8,128)(2,1)S(1)}, bf16[128,1536]{1,0:T(8,128)(2,1)}, u32[]{:S(2)}) copy-start(bf16[128,1536]{1,0:T(8,128)(2,1)} %refs_3_.1) | copy-start | bytes 1179652
  446.1 11.6 %copy-start.57 = (f32[128,1536]{1,0:T(8,128)S(1)}, f32[128,1536]{1,0:T(8,128)}, u32[]{:S(2)}) copy-start(f32[128,1536]{1,0:T(8,128)} %get-tuple-element.159) | copy-start | bytes 2359300
  454.3 13.4 %all-to-all-start.9 = ((bf16[8,48,384]{2,1,0:T(8,128)(2,1)}), bf16[8,48,384]{2,1,0:T(8,128)(2,1)S(1)}, u32[]{:S(2)}, u32[]{:S(2)}) async-start(bf16[8,48,384]{2,1,0:T(8,128)(2,1)} %reduce_sum.85), calls=%async_computation.9 | async-start | bytes 589824 | tf_op jit(solution)/shard_map/all_to_all | solution.py:933
  (44 other events, 59.2 us)
Sparse Core Ops, SparseCore 0:
  11.5 89.0 all-gather.2
  350.4 46.2 all-gather.4
  443.7 26.7 reduce-scatter.1
where the time goes:
time: 481 us; the launch traced here: 479 us
  waiting for transfers between devices  179 us (37%)
  starting transfers between devices  83.1 us (17%)
  Pallas kernels  66 us (14%)
  local copies, waits for them, and re-layouts  57.3 us (12%)
  blocking collectives  35.7 us (7%)
  other arithmetic  23 us (5%)
  matrix products  19.9 us (4%)
  between operations  14.7 us (3%)
    unnamed x135, local copies, waits for them, and re-layouts  41.7 us
    ppermute x3, waiting for transfers between devices, line_gather(): up = lax.ppermute(up, 'hg', [(m, m + 1) for m in range(turn, last)])  36.1 us
    all_to_all x1, blocking collectives, exchange(): lax.all_to_all(rows.reshape(experts, capacity, rows.shape[1]), BLK, split...  35.7 us
    ppermute x3, waiting for transfers between devices, line_gather(): lax.ppermute(down, 'hg', [(m, m - 1) for m in range(last - turn, 0, -1)])  28.4 us
    all_to_all x3, waiting for transfers between devices, exchange(): lax.all_to_all(rows.reshape(experts, capacity, rows.shape[1]), BLK, split...  22.5 us
    all_to_all x1, waiting for transfers between devices, shards(): lax.all_to_all(jnp.broadcast_to(slab_team[None], (planes, in_group, rows_...  16.3 us
    ppermute x3, starting transfers between devices, line_sum(): up = lax.ppermute(to_up, 'hg', [(m, m + 1) for m in range(turn + 1)])  14.9 us
    pallas_call x1, Pallas kernels, attend_back(): pl.pallas_call(functools.partial(attend_back_kernel, segments=lengths.sha...  14.8 us
  transfers between devices with their start and end apart: 42, of which 23 were waited for; matrix products, arithmetic and copies ran while one was open for 10% of the time, Pallas kernels for 8%

commit v1 on v0

--- a/solution.py
+++ b/solution.py
@@ -238,7 +238,6 @@
         compiler_params=pltpu.CompilerParams(
             vmem_limit_bytes=math.prod(whole) * 6 + (10 << 20)
         ),
-        name="attend",
     )(lengths, meta, query, *pieces)
 
 
@@ -254,7 +253,6 @@
         compiler_params=pltpu.CompilerParams(
             vmem_limit_bytes=math.prod(whole) * 14 + (10 << 20)
         ),
-        name="attend_back",
     )(lengths, meta, query, d_out, out, lse, *pieces)
 
 
@@ -319,7 +317,6 @@
             pltpu.SemaphoreType.DMA((len(pieces),)),
         ],
         compiler_params=pltpu.CompilerParams(vmem_limit_bytes=planes * rows * KV * 4 + (16 << 20)),
-        name="project",
     )(place, *pieces, slab)
 
 
@@ -370,7 +367,6 @@
         grad_in_kernel,
         out_shape=jax.ShapeDtypeStruct((planes, team, rows, width), BF16),
         compiler_params=pltpu.CompilerParams(vmem_limit_bytes=16 << 20),
-        name="grad_in",
     )(normed, d_qkv, extras)
 
 
@@ -390,7 +386,6 @@
         attn_back_kernel,
         out_shape=jax.ShapeDtypeStruct(d_proj.shape, BF16),
         compiler_params=pltpu.CompilerParams(vmem_limit_bytes=10 << 20),
-        name="attn_back",
     )(d_proj, full_out)
 
 
@@ -494,7 +489,6 @@
             pltpu.SemaphoreType.DMA((4,)),
         ],
         compiler_params=pltpu.CompilerParams(vmem_limit_bytes=26 << 20),
-        name="expert",
     )(expert, x_own, x_other, d_own, d_other, gate, up, down)
 
 
@@ -523,7 +517,6 @@
         ],
         out_specs=pl.BlockSpec((step, width), lambda i: (i, 0)),
         compiler_params=pltpu.CompilerParams(vmem_limit_bytes=8 << 20),
-        name="pair_back",
     )(expert, partial, theirs)
 
 
@@ -567,7 +560,6 @@
             pl.BlockSpec((1, width, step), lambda i: (0, 0, i)),
         ],
         compiler_params=pltpu.CompilerParams(vmem_limit_bytes=24 << 20),
-        name="expert_grads",
     )(x_own, x_other, d_own, d_other, inner, d_gate, d_up)
 
 
@@ -625,7 +617,6 @@
             line,
         ),
         compiler_params=pltpu.CompilerParams(vmem_limit_bytes=8 << 20),
-        name="finish_grads",
     )(parts, by_group)
     return out[:4] + (out[4].reshape(rows), out[5].reshape(rows))
 
@@ -665,7 +656,6 @@
         in_specs=[pl.BlockSpec(memory_space=pltpu.SMEM)]
         + [pl.BlockSpec(memory_space=pltpu.VMEM)] * (planes + 2),
         compiler_params=pltpu.CompilerParams(vmem_limit_bytes=planes * rows * KV * 4 + (12 << 20)),
-        name="merge_back",
     )(turn, d_query, *d_kv_parts, slab)
 
 
@@ -683,7 +673,6 @@
             pl.BlockSpec(memory_space=pltpu.VMEM),
         ],
         compiler_params=pltpu.CompilerParams(vmem_limit_bytes=10 << 20),
-        name="slab_back",
     )(turn, d_qkv, slab)
 
 
@@ -874,10 +863,10 @@
     d_token = jnp.dot(token_table, d_back, preferred_element_type=F32)
     d_mix = d_token[:, D : D + experts] + d_token[:, D + experts : D + 2 * experts]
     d_logits = (mix * (d_mix - jnp.sum(mix * d_mix, axis=1, keepdims=True))).astype(BF16)
-    grad_router_part = jnp.einsum("td,te->de", normed_two, d_logits, preferred_element_type=F32)
     d_normed_two = d_token[:, :D] + jnp.einsum(
         "te,de->td", d_logits, router, preferred_element_type=F32
     )
+    grad_router_part = jnp.einsum("td,te->de", normed_two, d_logits, preferred_element_type=F32)
     gain_moe_part = lax.dot_general(
         d_normed_two * hidden_one,
         scale_two,
@@ -913,10 +902,9 @@
         "ti,td->id", attn_rows, d_proj_group, preferred_element_type=F32
     ).astype(BF16)
     grad_out = lax.psum_scatter(out_part, "tg", scatter_dimension=0, tiled=True).astype(F32)
-    d_kv_parts = [d_kv_sends[0]] + [
-        lax.ppermute(d_kv_sends[distance], "tg", next_planes(distance))
-        for distance in range(1, planes)
-    ]
+    d_kv_parts = [d_kv_sends[0]]
+    for distance in range(1, planes):
+        d_kv_parts.append(lax.ppermute(d_kv_sends[distance], "tg", next_planes(distance)))
     d_kv_parts = [part.reshape(rows_group, KV) for part in d_kv_parts]
     head = lax.axis_index("head")
     turns = jnp.stack([heads - 1 - head, head]).astype(jnp.int32)

time: 481 us -> 481 us (level)
  no operation moved by 1% of the time
where the time goes in v1:
time: 481 us; the launch traced here: 479 us
  waiting for transfers between devices  179 us (37%)
  starting transfers between devices  83.1 us (17%)
  Pallas kernels  66 us (14%)
  local copies, waits for them, and re-layouts  57.3 us (12%)
  blocking collectives  35.7 us (7%)
  other arithmetic  23 us (5%)
  matrix products  19.9 us (4%)
  between operations  14.7 us (3%)
    unnamed x135, local copies, waits for them, and re-layouts  41.7 us
    ppermute x3, waiting for transfers between devices, line_gather(): up = lax.ppermute(up, 'hg', [(m, m + 1) for m in range(turn, last)])  36.1 us
    all_to_all x1, blocking collectives, exchange(): lax.all_to_all(rows.reshape(experts, capacity, rows.shape[1]), BLK, split...  35.7 us
    ppermute x3, waiting for transfers between devices, line_gather(): lax.ppermute(down, 'hg', [(m, m - 1) for m in range(last - turn, 0, -1)])  28.4 us
    all_to_all x3, waiting for transfers between devices, exchange(): lax.all_to_all(rows.reshape(experts, capacity, rows.shape[1]), BLK, split...  22.5 us
    all_to_all x1, waiting for transfers between devices, shards(): lax.all_to_all(jnp.broadcast_to(slab_team[None], (planes, in_group, rows_...  16.3 us
    ppermute x3, starting transfers between devices, line_sum(): up = lax.ppermute(to_up, 'hg', [(m, m + 1) for m in range(turn + 1)])  14.9 us
    pallas_call x1, Pallas kernels, attend_back(): pl.pallas_call(functools.partial(attend_back_kernel, segments=lengths.sha...  14.8 us
  transfers between devices with their start and end apart: 42, of which 23 were waited for; matrix products, arithmetic and copies ran while one was open for 10% of the time, Pallas kernels for 8%

profile of v1, /device:TPU:0, one launch (start us, length us, event | category | flops | bytes accessed | tf_op | source)
XLA Modules:
  0.0 478.7 jit_solution(17038087123997231487)
XLA Ops:
  8.8 1.7 concatenate.13
  13.8 6.4 %all-to-all-start.1 = ((bf16[8,48,384]{2,1,0:T(8,128)(2,1)}), bf16[8,48,384]{2,1,0:T(8,128)(2,1)S(1)}, u32[]{:S(2)}, u32[]{:S(2)}) async-start(bf16[8,48,384]{2,1,0:T(8,128)(2,1)} %bitcast.8.slab_ref), calls=%async_computation.1 | async-start | bytes 589824 | tf_op jit(solution)/shard_map/all_to_all | solution.py:747
  22.1 10.0 %all-to-all-done.1 = bf16[8,48,384]{2,1,0:T(8,128)(2,1)S(1)} async-done(((bf16[8,48,384]{2,1,0:T(8,128)(2,1)}), bf16[8,48,384]{2,1,0:T(8,128)(2,1)S(1)}, u32[]{:S(2)}, u32[]{:S(2)}) %all-to-all-start.1) | async-done | bytes 294944 | tf_op jit(solution)/shard_map/all_to_all | solution.py:747
  33.3 4.0 all-to-all-start.2
  41.4 16.3 %all-to-all-done.2.refs_14_ = bf16[4,8,48,384]{3,2,1,0:T(8,128)(2,1)S(1)} async-done(((bf16[4,8,48,384]{3,2,1,0:T(8,128)(2,1)}), bf16[4,8,48,384]{3,2,1,0:T(8,128)(2,1)S(1)}, u32[]{:S(2)}, u32[]{:S(2)}) %all-to-all-start.2) | async-done | bytes 1179680 | tf_op jit(solution)/shard_map/all_to_all | solution.py:750
  57.7 3.7 all-to-all-start
  61.4 3.8 collective-permute-start
  66.5 36.1 %collective-permute-done.refs_2_ = bf16[128,1536]{1,0:T(8,128)(2,1)S(1)} collective-permute-done((bf16[128,1536]{1,0:T(8,128)(2,1)S(1)}, bf16[128,1536]{1,0:T(8,128)(2,1)S(1)}, u32[]{:S(2)}, u32[]{:S(2)}) %collective-permute-start) | collective-permute-done | bytes 393248 | tf_op jit(solution)/shard_map/ppermute | solution.py:330
  102.5 2.1 collective-permute-done.1.refs_4_
  106.6 17.9 %collective-permute-done.3.refs_5_ = bf16[128,1536]{1,0:T(8,128)(2,1)S(1)} collective-permute-done((bf16[128,1536]{1,0:T(8,128)(2,1)S(1)}, bf16[128,1536]{1,0:T(8,128)(2,1)S(1)}, u32[]{:S(2)}, u32[]{:S(2)}) %collective-permute-start.3) | collective-permute-done | bytes 393248 | tf_op jit(solution)/shard_map/ppermute | solution.py:331
  127.6 8.4 %collective-permute-done.5.refs_6_ = bf16[128,1536]{1,0:T(8,128)(2,1)S(1)} collective-permute-done((bf16[128,1536]{1,0:T(8,128)(2,1)S(1)}, bf16[128,1536]{1,0:T(8,128)(2,1)S(1)}, u32[]{:S(2)}, u32[]{:S(2)}) %collective-permute-start.5) | collective-permute-done | bytes 393248 | tf_op jit(solution)/shard_map/ppermute | solution.py:331
  138.9 7.1 %shard_map.229 = (bf16[1024,1536]{1,0:T(8,128)(2,1)S(1)}, bf16[1024,192]{1,0:T(8,128)(2,1)S(1)}, bf16[1024,128]{1,0:T(8,128)(2,1)S(1)}, bf16[1536,384]{1,0:T(8,128)(2,1)S(1)}, f32[1,1536]{1,0:T(1,128)S(1)}) custom-call(s32[2]{0:T(128)S(1)} %pad_add_fusion.place_ref, bf16[128,1536]{1,0:T(8,128)(2,1)S(1)} %collective-permute-done.4.refs_0_, ...), custom_call_target="tpu_custom_call" | custom-call | tf_op jit(solution)/shard_map/pallas_call | solution.py:303
  147.0 1.8 copy-done.15
  150.3 2.5 collective-permute-start.14
  154.2 5.2 %collective-permute-done.13.refs_1_ = bf16[8,128,128]{2,1,0:T(8,128)(2,1)S(1)} collective-permute-done((bf16[8,128,128]{2,1,0:T(8,128)(2,1)S(1)}, bf16[8,128,128]{2,1,0:T(8,128)(2,1)S(1)}, u32[]{:S(2)}, u32[]{:S(2)}) %collective-permute-start.13) | collective-permute-done | bytes 262176 | tf_op jit(solution)/shard_map/ppermute | solution.py:823
  159.4 5.0 %collective-permute-done.14.refs_2_ = bf16[8,128,128]{2,1,0:T(8,128)(2,1)S(1)} collective-permute-done((bf16[8,128,128]{2,1,0:T(8,128)(2,1)S(1)}, bf16[8,128,128]{2,1,0:T(8,128)(2,1)S(1)}, u32[]{:S(2)}, u32[]{:S(2)}) %collective-permute-start.14) | collective-permute-done | bytes 262176 | tf_op jit(solution)/shard_map/ppermute | solution.py:823
  164.8 11.3 %shard_map.230 = (bf16[1024,192]{1,0:T(8,128)(2,1)S(1)}, f32[8,1,384]{2,1,0:T(1,128)S(1)}) custom-call(s32[12]{0:T(128)S(1)} %copy-done.41, s32[1]{0:T(128)} %bitcast.5.meta_ref, bf16[1024,192]{1,0:T(8,128)(2,1)S(1)} %get-tuple-element.65.q_ref, bf16[8,128,128]{2,1,0:T(8,128)(2,1)S(1)} %bitcast.112, ...), custom_call_target="tpu_custom_call" | custom-call | tf_op jit(solution)/shard_map/pallas_call | solution.py:230
  180.7 3.5 all-to-all-start.3
  184.2 11.9 %all-to-all-done.3 = bf16[8,128,192]{1,2,0:T(8,128)(2,1)S(1)} async-done(((bf16[8,128,192]{1,2,0:T(8,128)(2,1)}), bf16[8,128,192]{1,2,0:T(8,128)(2,1)S(1)}, u32[]{:S(2)}, u32[]{:S(2)}) %all-to-all-start.3) | async-done | bytes 393248 | tf_op jit(solution)/shard_map/all_to_all | solution.py:830
  196.1 3.2 multiply_reduce_fusion.1
  203.7 35.7 %all_to_all.78 = bf16[16,24,1664]{2,1,0:T(8,128)(2,1)S(1)} all-to-all(bf16[16,24,1664]{2,1,0:T(8,128)(2,1)S(1)} %bitcast.123), channel_id=1, replica_groups=mesh['head'=2,'hg'=4,'tg'=4] {'hg','tg'}, dimensions={0} | all-to-all | bytes 2555904 | tf_op jit(solution)/shard_map/all_to_all | solution.py:798
  239.9 4.2 collective-permute-done.17.d_other_ref
  244.1 2.3 copy-done.23
  246.4 10.1 %shard_map.231 = (bf16[768,1664]{1,0:T(8,128)(2,1)S(1)}, bf16[768,512]{1,0:T(8,128)(2,1)S(1)}, bf16[768,512]{1,0:T(8,128)(2,1)S(1)}, bf16[768,512]{1,0:T(8,128)(2,1)S(1)}) custom-call(s32[1]{0:T(128)} %bitcast.15.expert_ref, bf16[384,1664]{1,0:T(8,128)(2,1)S(1)} %bitcast.98, bf16[384,1664]{1,0:T(8,128)(2,1)S(1)} %collective-permute-done.16.x_other_ref, ...), custom_call_target="tpu_custom_call" | custom-call | tf_op jit(solution)/shard_map/pallas_call | solution.py:480
  256.9 2.9 collective-permute-done.18.other_ref
  261.7 4.6 all-to-all-start.5
  266.3 3.0 fusion.39
  269.3 2.2 copy-done.49
  272.8 22.5 %all-to-all-done.5 = bf16[16,24,1664]{2,1,0:T(8,128)(2,1)} async-done(((bf16[16,24,1664]{2,1,0:T(8,128)(2,1)}), bf16[16,24,1664]{2,1,0:T(8,128)(2,1)}, u32[]{:S(2)}, u32[]{:S(2)}) %all-to-all-start.5) | async-done | bytes 1277984 | tf_op jit(solution)/shard_map/all_to_all | solution.py:798
  295.3 1.8 fusion.23
  300.1 2.6 copy-done
  302.7 2.0 shard_map.233
  305.5 1.9 copy.78
  307.4 5.6 %all-to-all-start.6 = ((bf16[128,8,192]{0,2,1:T(8,128)(2,1)}), bf16[128,8,192]{0,2,1:T(8,128)(2,1)S(1)}, u32[]{:S(2)}, u32[]{:S(2)}) async-start(bf16[128,8,192]{0,2,1:T(8,128)(2,1)} %bitcast.127), calls=%async_computation.6 | async-start | bytes 786432 | tf_op jit(solution)/shard_map/all_to_all | solution.py:895
  313.1 3.3 fusion.7
  316.5 8.6 %all-to-all-done.6 = bf16[128,8,192]{0,2,1:T(8,128)(2,1)S(1)} async-done(((bf16[128,8,192]{0,2,1:T(8,128)(2,1)}), bf16[128,8,192]{0,2,1:T(8,128)(2,1)S(1)}, u32[]{:S(2)}, u32[]{:S(2)}) %all-to-all-start.6) | async-done | bytes 393248 | tf_op jit(solution)/shard_map/all_to_all | solution.py:895
  331.8 14.8 %shard_map.234 = (bf16[1024,192]{1,0:T(8,128)(2,1)S(1)}, bf16[8,128,128]{2,1,0:T(8,128)(2,1)S(1)}, bf16[8,128,128]{2,1,0:T(8,128)(2,1)S(1)}, bf16[8,128,128]{2,1,0:T(8,128)(2,1)S(1)}, bf16[8,128,128]{2,1,0:T(8,128)(2,1)S(1)}) custom-call(s32[12]{0:T(128)S(1)} %copy-done.41, s32[1]{0:T(128)} %bitcast.5.meta_ref, bf16[1024,192]{1,0:T(8,128)(2,1)S(1)} %copy-done.21, ...), custom_call_target="tpu_custom_call" | custom-call | tf_op jit(solution)/shard_map/pallas_call | solution.py:248
  350.3 4.0 collective-permute-start.21
  354.4 2.8 collective-permute-start.22
  357.2 3.5 collective-permute-done.20
  360.7 5.7 %collective-permute-done.21 = bf16[8,128,128]{2,1,0:T(8,128)(2,1)S(1)} collective-permute-done((bf16[8,128,128]{2,1,0:T(8,128)(2,1)}, bf16[8,128,128]{2,1,0:T(8,128)(2,1)S(1)}, u32[]{:S(2)}, u32[]{:S(2)}) %collective-permute-start.21) | collective-permute-done | bytes 262176 | tf_op jit(solution)/shard_map/ppermute | solution.py:907
  366.4 1.9 collective-permute-done.22
  371.5 3.7 shard_map.235
  376.2 4.4 all-to-all-start.7
  384.2 1.8 add_convert_fusion
  388.0 4.5 collective-permute-start.24
  399.9 9.1 %shard_map.239 = (f32[1,1536,512]{2,1,0:T(8,128)}, f32[1,1536,512]{2,1,0:T(8,128)}, f32[1,512,1536]{2,1,0:T(8,128)}) custom-call(bf16[384,1664]{1,0:T(8,128)(2,1)S(1)} %bitcast.99, bf16[384,1664]{1,0:T(8,128)(2,1)S(1)} %copy-done.3, bf16[384,1536]{1,0:T(8,128)(2,1)S(1)} %bitcast.102, bf16[384,1536]{1,0:T(8,128)(2,1)S(1)} %copy-done.6, ...), custom_call_target="tpu_custom_call" | custom-call | tf_op jit(solution)/shard_map/pallas_call | solution.py:548
  409.5 2.0 collective-permute-done.24
  411.6 2.2 fusion.13
  413.8 5.2 %collective-permute-start.26 = (bf16[128,1536]{1,0:T(8,128)(2,1)}, bf16[128,1536]{1,0:T(8,128)(2,1)}, u32[]{:S(2)}, u32[]{:S(2)}) collective-permute-start(bf16[128,1536]{1,0:T(8,128)(2,1)} %get-tuple-element.165), channel_id=1, source_target_pairs={{0,4},{4,8},{1,5},{5,9},{2,6},{6,10},{3,7},{7,11},{16,20},{20,24},... | collective-permute-start | bytes 1179656 | tf_op jit(solution)/shard_map/ppermute | solution.py:693
  421.3 1.9 copy-done.16
  423.2 3.5 shard_map.237
  426.7 4.4 all-to-all-start.8
  431.2 2.2 fusion.12
  433.4 5.3 %collective-permute-start.28 = (bf16[128,1536]{1,0:T(8,128)(2,1)}, bf16[128,1536]{1,0:T(8,128)(2,1)}, u32[]{:S(2)}, u32[]{:S(2)}) collective-permute-start(bf16[128,1536]{1,0:T(8,128)(2,1)} %get-tuple-element.163), channel_id=1, source_target_pairs={{0,4},{4,8},{8,12},{1,5},{5,9},{9,13},{2,6},{6,10},{10,14},{3,7},{... | collective-permute-start | bytes 1179656 | tf_op jit(solution)/shard_map/ppermute | solution.py:693
  440.1 3.5 convolution_convert_fusion.2
  443.6 2.5 fusion.6
  446.1 4.4 collective-permute-done.29
  452.1 2.2 reduce_sum.85
  454.3 3.4 all-to-all-start.9
  457.8 2.2 fusion.11
  459.9 7.8 %all-to-all-done.9.parts_ref = bf16[8,48,384]{2,1,0:T(8,128)(2,1)S(1)} async-done(((bf16[8,48,384]{2,1,0:T(8,128)(2,1)}), bf16[8,48,384]{2,1,0:T(8,128)(2,1)S(1)}, u32[]{:S(2)}, u32[]{:S(2)}) %all-to-all-start.9) | async-done | bytes 294944 | tf_op jit(solution)/shard_map/all_to_all | solution.py:921
  467.7 2.2 shard_map.238
  470.6 1.6 convert_element_type.190
  (247 shorter events, 76.2 us)
Async XLA Ops:
  7.2 5.4 %copy-start.63 = (bf16[48,512]{1,0:T(8,128)(2,1)S(1)}, bf16[48,512]{1,0:T(8,128)(2,1)}, u32[]{:S(2)}) copy-start(bf16[48,512]{1,0:T(8,128)(2,1)} %param.19) | copy-start | bytes 147460
  7.2 5.6 %copy-start.65 = (bf16[48]{0:T(256)(128)(2,1)S(1)}, bf16[48]{0:T(256)(128)(2,1)}, u32[]{:S(2)}) copy-start(bf16[48]{0:T(256)(128)(2,1)} %param.22) | copy-start | bytes 292
  7.2 188.9 %all-gather.3.cloned.1.call-start = ((), (), s32[]{:S(2)}) async-start(), calls=%async_computation.11 | async-start | bytes 5271552 | tf_op jit(solution)/shard_map/all_gather | solution.py:767
  10.5 9.7 %copy-start.64 = (s32[128,2]{0,1:T(2,128)S(1)}, s32[128,2]{0,1:T(2,128)}, u32[]{:S(2)}) copy-start(s32[128,2]{0,1:T(2,128)} %param.16) | copy-start | bytes 3076
  10.5 9.8 %copy-start.41 = (s32[12]{0:T(128)S(1)}, s32[12]{0:T(128)}, u32[]{:S(2)}) copy-start(s32[12]{0:T(128)} %lengths_ref.3) | copy-start | bytes 148
  13.8 18.3 %all-to-all-start.1 = ((bf16[8,48,384]{2,1,0:T(8,128)(2,1)}), bf16[8,48,384]{2,1,0:T(8,128)(2,1)S(1)}, u32[]{:S(2)}, u32[]{:S(2)}) async-start(bf16[8,48,384]{2,1,0:T(8,128)(2,1)} %bitcast.8.slab_ref), calls=%async_computation.1 | async-start | bytes 589824 | tf_op jit(solution)/shard_map/all_to_all | solution.py:747
  33.3 6.5 %copy-start.58 = (bf16[128,1536]{1,0:T(8,128)(2,1)S(1)}, bf16[128,1536]{1,0:T(8,128)(2,1)}, u32[]{:S(2)}) copy-start(bf16[128,1536]{1,0:T(8,128)(2,1)} %param.27) | copy-start | bytes 1179652
  33.3 24.4 %all-to-all-start.2 = ((bf16[4,8,48,384]{3,2,1,0:T(8,128)(2,1)}), bf16[4,8,48,384]{3,2,1,0:T(8,128)(2,1)S(1)}, u32[]{:S(2)}, u32[]{:S(2)}) async-start(bf16[4,8,48,384]{3,2,1,0:T(8,128)(2,1)} %broadcast_in_dim.59), calls=%async_computation.2 | async-start | bytes 2359296 | tf_op jit(solution)/shard_map/all_to_all | solution.py:750
  41.4 20.0 %copy-start.11 = (bf16[128,1536]{1,0:T(8,128)(2,1)S(1)}, bf16[128,1536]{1,0:T(8,128)(2,1)}, u32[]{:S(2)}) copy-start(bf16[128,1536]{1,0:T(8,128)(2,1)} %refs_3_.1) | copy-start | bytes 1179652
  57.7 122.1 %all-to-all-start = ((bf16[16,24,1536]{2,1,0:T(8,128)(2,1)}), bf16[16,24,1536]{2,1,0:T(8,128)(2,1)S(1)}, u32[]{:S(2)}, u32[]{:S(2)}) async-start(bf16[16,24,1536]{2,1,0:T(8,128)(2,1)} %bitcast.124), calls=%async_computation | async-start | bytes 2359296 | tf_op jit(solution)/shard_map/all_to_all | solution.py:798
  61.4 41.1 %collective-permute-start = (bf16[128,1536]{1,0:T(8,128)(2,1)S(1)}, bf16[128,1536]{1,0:T(8,128)(2,1)S(1)}, u32[]{:S(2)}, u32[]{:S(2)}) collective-permute-start(bf16[128,1536]{1,0:T(8,128)(2,1)S(1)} %copy-done.11), channel_id=1, source_target_pairs={{0,4},{4,8},{8,12},{1,5},{5,9},{9,13},{2,6},{6,10},{10,14},{3,7},{... | collective-permute-start | bytes 1179656 | tf_op jit(solution)/shard_map/ppermute | solution.py:330
  65.2 39.5 %collective-permute-start.1 = (bf16[128,1536]{1,0:T(8,128)(2,1)S(1)}, bf16[128,1536]{1,0:T(8,128)(2,1)S(1)}, u32[]{:S(2)}, u32[]{:S(2)}) collective-permute-start(bf16[128,1536]{1,0:T(8,128)(2,1)S(1)} %copy-done.11), channel_id=1, source_target_pairs={{12,8},{8,4},{4,0},{13,9},{9,5},{5,1},{14,10},{10,6},{6,2},{15,11}... | collective-permute-start | bytes 1179656 | tf_op jit(solution)/shard_map/ppermute | solution.py:331
  104.6 2.0 collective-permute-start.2
  105.3 19.2 %collective-permute-start.3 = (bf16[128,1536]{1,0:T(8,128)(2,1)S(1)}, bf16[128,1536]{1,0:T(8,128)(2,1)S(1)}, u32[]{:S(2)}, u32[]{:S(2)}) collective-permute-start(bf16[128,1536]{1,0:T(8,128)(2,1)S(1)} %collective-permute-done.1.refs_4_), channel_id=1, source_target_pairs={{8,4},{4,0},{9,5},{5,1},{10,6},{6,2},{11,7},{7,3},{24,20},{20,16},... | collective-permute-start | bytes 1179656 | tf_op jit(solution)/shard_map/ppermute | solution.py:331
  124.5 2.6 collective-permute-start.4
  125.2 10.8 %collective-permute-start.5 = (bf16[128,1536]{1,0:T(8,128)(2,1)S(1)}, bf16[128,1536]{1,0:T(8,128)(2,1)S(1)}, u32[]{:S(2)}, u32[]{:S(2)}) collective-permute-start(bf16[128,1536]{1,0:T(8,128)(2,1)S(1)} %collective-permute-done.3.refs_5_), channel_id=1, source_target_pairs={{4,0},{5,1},{6,2},{7,3},{20,16},{21,17},{22,18},{23,19}} | collective-permute-start | bytes 1179656 | tf_op jit(solution)/shard_map/ppermute | solution.py:331
  126.5 9.5 %collective-permute-start.9 = (bf16[128,1536]{1,0:T(8,128)(2,1)S(1)}, bf16[128,1536]{1,0:T(8,128)(2,1)S(1)}, u32[]{:S(2)}, u32[]{:S(2)}) collective-permute-start(bf16[128,1536]{1,0:T(8,128)(2,1)S(1)} %copy-done.11), channel_id=1, source_target_pairs={{0,16},{16,0},{1,17},{17,1},{2,18},{18,2},{3,19},{19,3},{4,20},{20... | collective-permute-start | bytes 1179656 | tf_op jit(solution)/shard_map/ppermute | solution.py:327
  126.6 9.9 %collective-permute-start.8 = (bf16[128,1536]{1,0:T(8,128)(2,1)S(1)}, bf16[128,1536]{1,0:T(8,128)(2,1)S(1)}, u32[]{:S(2)}, u32[]{:S(2)}) collective-permute-start(bf16[128,1536]{1,0:T(8,128)(2,1)S(1)} %collective-permute-done.refs_2_), channel_id=1, source_target_pairs={{0,16},{16,0},{1,17},{17,1},{2,18},{18,2},{3,19},{19,3},{4,20},{20... | collective-permute-start | bytes 1179656 | tf_op jit(solution)/shard_map/ppermute | solution.py:334
  127.1 9.6 %collective-permute-start.10 = (bf16[128,1536]{1,0:T(8,128)(2,1)S(1)}, bf16[128,1536]{1,0:T(8,128)(2,1)S(1)}, u32[]{:S(2)}, u32[]{:S(2)}) collective-permute-start(bf16[128,1536]{1,0:T(8,128)(2,1)S(1)} %collective-permute-done.1.refs_4_), channel_id=1, source_target_pairs={{0,16},{16,0},{1,17},{17,1},{2,18},{18,2},{3,19},{19,3},{4,20},{20... | collective-permute-start | bytes 1179656 | tf_op jit(solution)/shard_map/ppermute | solution.py:335
  127.2 9.5 %collective-permute-start.7 = (bf16[128,1536]{1,0:T(8,128)(2,1)S(1)}, bf16[128,1536]{1,0:T(8,128)(2,1)S(1)}, u32[]{:S(2)}, u32[]{:S(2)}) collective-permute-start(bf16[128,1536]{1,0:T(8,128)(2,1)S(1)} %collective-permute-done.2.refs_1_), channel_id=1, source_target_pairs={{0,16},{16,0},{1,17},{17,1},{2,18},{18,2},{3,19},{19,3},{4,20},{20... | collective-permute-start | bytes 1179656 | tf_op jit(solution)/shard_map/ppermute | solution.py:334
  136.0 1.7 collective-permute-start.11
  136.0 2.3 collective-permute-start.6
  136.5 2.3 collective-permute-start.12
  148.8 10.6 %collective-permute-start.13 = (bf16[8,128,128]{2,1,0:T(8,128)(2,1)S(1)}, bf16[8,128,128]{2,1,0:T(8,128)(2,1)S(1)}, u32[]{:S(2)}, u32[]{:S(2)}) collective-permute-start(bf16[8,128,128]{2,1,0:T(8,128)(2,1)S(1)} %bitcast.109), channel_id=1, source_target_pairs={{0,1},{1,2},{2,3},{3,0},{4,5},{5,6},{6,7},{7,4},{8,9},{9,10},{10,1... | collective-permute-start | bytes 786440 | tf_op jit(solution)/shard_map/ppermute | solution.py:823
  150.3 14.2 %collective-permute-start.14 = (bf16[8,128,128]{2,1,0:T(8,128)(2,1)S(1)}, bf16[8,128,128]{2,1,0:T(8,128)(2,1)S(1)}, u32[]{:S(2)}, u32[]{:S(2)}) collective-permute-start(bf16[8,128,128]{2,1,0:T(8,128)(2,1)S(1)} %bitcast.110), channel_id=1, source_target_pairs={{0,2},{1,3},{2,0},{3,1},{4,6},{5,7},{6,4},{7,5},{8,10},{9,11},{10,... | collective-permute-start | bytes 786440 | tf_op jit(solution)/shard_map/ppermute | solution.py:823
  152.8 12.0 %collective-permute-start.15 = (bf16[8,128,128]{2,1,0:T(8,128)(2,1)S(1)}, bf16[8,128,128]{2,1,0:T(8,128)(2,1)S(1)}, u32[]{:S(2)}, u32[]{:S(2)}) collective-permute-start(bf16[8,128,128]{2,1,0:T(8,128)(2,1)S(1)} %bitcast.111), channel_id=1, source_target_pairs={{0,3},{1,0},{2,1},{3,2},{4,7},{5,4},{6,5},{7,6},{8,11},{9,8},{10,9... | collective-permute-start | bytes 786440 | tf_op jit(solution)/shard_map/ppermute | solution.py:823
  180.7 15.4 %all-to-all-start.3 = ((bf16[8,128,192]{1,2,0:T(8,128)(2,1)}), bf16[8,128,192]{1,2,0:T(8,128)(2,1)S(1)}, u32[]{:S(2)}, u32[]{:S(2)}) async-start(bf16[8,128,192]{1,2,0:T(8,128)(2,1)} %copy.74), calls=%async_computation.3 | async-start | bytes 786432 | tf_op jit(solution)/shard_map/all_to_all | solution.py:830
  203.0 41.1 %copy-start.22 = (bf16[1,1536,512]{2,1,0:T(8,128)(2,1)S(1)}, bf16[1,1536,512]{2,1,0:T(8,128)(2,1)}, u32[]{:S(2)}) copy-start(bf16[1,1536,512]{2,1,0:T(8,128)(2,1)} %param.24) | copy-start | bytes 4718596
  203.7 40.4 %copy-start.1 = (bf16[1,512,1536]{2,1,0:T(8,128)(2,1)S(1)}, bf16[1,512,1536]{2,1,0:T(8,128)(2,1)}, u32[]{:S(2)}) copy-start(bf16[1,512,1536]{2,1,0:T(8,128)(2,1)} %param.26) | copy-start | bytes 4718596
  239.4 4.7 collective-permute-start.16
  239.4 4.7 collective-permute-start.17
  244.1 12.4 %copy-start.5 = (bf16[384,1536]{1,0:T(8,128)(2,1)}, bf16[384,1536]{1,0:T(8,128)(2,1)S(1)}, u32[]{:S(2)}) copy-start(bf16[384,1536]{1,0:T(8,128)(2,1)S(1)} %collective-permute-done.17.d_other_ref) | copy-start | bytes 3538948
  244.1 12.4 %copy-start.2 = (bf16[384,1664]{1,0:T(8,128)(2,1)}, bf16[384,1664]{1,0:T(8,128)(2,1)S(1)}, u32[]{:S(2)}) copy-start(bf16[384,1664]{1,0:T(8,128)(2,1)S(1)} %collective-permute-done.16.x_other_ref) | copy-start | bytes 3833860
  256.5 4.1 copy-start.13
  256.6 4.1 copy-start.33
  256.6 4.1 copy-start.35
  256.7 3.1 collective-permute-start.18
  261.7 33.6 %all-to-all-start.5 = ((bf16[16,24,1664]{2,1,0:T(8,128)(2,1)}), bf16[16,24,1664]{2,1,0:T(8,128)(2,1)}, u32[]{:S(2)}, u32[]{:S(2)}) async-start(bf16[16,24,1664]{2,1,0:T(8,128)(2,1)} %bitcast.104), calls=%async_computation.5 | async-start | bytes 2555904 | tf_op jit(solution)/shard_map/all_to_all | solution.py:798
  272.7 40.4 %collective-permute-start.19 = (bf16[384,1536]{1,0:T(8,128)(2,1)}, bf16[384,1536]{1,0:T(8,128)(2,1)}, u32[]{:S(2)}, u32[]{:S(2)}) collective-permute-start(bf16[384,1536]{1,0:T(8,128)(2,1)} %slice.106), channel_id=1, source_target_pairs={{0,16},{16,0},{1,17},{17,1},{2,18},{18,2},{3,19},{19,3},{4,20},{20... | collective-permute-start | bytes 3538952 | tf_op jit(solution)/shard_map/ppermute | solution.py:856
  300.1 4.6 copy-start.10
  307.4 17.6 %all-to-all-start.6 = ((bf16[128,8,192]{0,2,1:T(8,128)(2,1)}), bf16[128,8,192]{0,2,1:T(8,128)(2,1)S(1)}, u32[]{:S(2)}, u32[]{:S(2)}) async-start(bf16[128,8,192]{0,2,1:T(8,128)(2,1)} %bitcast.127), calls=%async_computation.6 | async-start | bytes 786432 | tf_op jit(solution)/shard_map/all_to_all | solution.py:895
  313.1 127.0 %all-gather.5.cloned.1.call-start = ((), (), s32[]{:S(2)}) async-start(), calls=%async_computation.12 | async-start | bytes 3538944 | tf_op jit(solution)/shard_map/all_gather | solution.py:900
  350.3 10.4 %collective-permute-start.20 = (bf16[8,128,128]{2,1,0:T(8,128)(2,1)}, bf16[8,128,128]{2,1,0:T(8,128)(2,1)S(1)}, u32[]{:S(2)}, u32[]{:S(2)}) collective-permute-start(bf16[8,128,128]{2,1,0:T(8,128)(2,1)} %copy-done.44), channel_id=1, source_target_pairs={{0,1},{1,2},{2,3},{3,0},{4,5},{5,6},{6,7},{7,4},{8,9},{9,10},{10,1... | collective-permute-start | bytes 786440 | tf_op jit(solution)/shard_map/ppermute | solution.py:907
  350.3 16.0 %collective-permute-start.21 = (bf16[8,128,128]{2,1,0:T(8,128)(2,1)}, bf16[8,128,128]{2,1,0:T(8,128)(2,1)S(1)}, u32[]{:S(2)}, u32[]{:S(2)}) collective-permute-start(bf16[8,128,128]{2,1,0:T(8,128)(2,1)} %copy-done.43), channel_id=1, source_target_pairs={{0,2},{1,3},{2,0},{3,1},{4,6},{5,7},{6,4},{7,5},{8,10},{9,11},{10,... | collective-permute-start | bytes 786440 | tf_op jit(solution)/shard_map/ppermute | solution.py:907
  354.4 13.9 %collective-permute-start.22 = (bf16[8,128,128]{2,1,0:T(8,128)(2,1)}, bf16[8,128,128]{2,1,0:T(8,128)(2,1)}, u32[]{:S(2)}, u32[]{:S(2)}) collective-permute-start(bf16[8,128,128]{2,1,0:T(8,128)(2,1)} %copy-done.42), channel_id=1, source_target_pairs={{0,3},{1,0},{2,1},{3,2},{4,7},{5,4},{6,5},{7,6},{8,11},{9,8},{10,9... | collective-permute-start | bytes 786440 | tf_op jit(solution)/shard_map/ppermute | solution.py:907
  376.2 8.0 %collective-permute-start.23 = (bf16[512,1536]{1,0:T(8,128)(2,1)}, bf16[512,1536]{1,0:T(8,128)(2,1)}, u32[]{:S(2)}, u32[]{:S(2)}) collective-permute-start(bf16[512,1536]{1,0:T(8,128)(2,1)} %get-tuple-element.85), channel_id=1, source_target_pairs={{0,16},{16,0},{1,17},{17,1},{2,18},{18,2},{3,19},{19,3},{4,20},{20... | collective-permute-start | bytes 4718600 | tf_op jit(solution)/shard_map/ppermute | solution.py:912
  376.2 45.1 %all-to-all-start.7 = ((bf16[16,24,1536]{2,1,0:T(8,128)(2,1)}), bf16[16,24,1536]{2,1,0:T(8,128)(2,1)}, u32[]{:S(2)}, u32[]{:S(2)}) async-start(bf16[16,24,1536]{2,1,0:T(8,128)(2,1)} %bitcast.125), calls=%async_computation.7 | async-start | bytes 2359296 | tf_op jit(solution)/shard_map/all_to_all | solution.py:798
  388.0 23.6 %collective-permute-start.24 = (bf16[128,1536]{1,0:T(8,128)(2,1)}, bf16[128,1536]{1,0:T(8,128)(2,1)}, u32[]{:S(2)}, u32[]{:S(2)}) collective-permute-start(bf16[128,1536]{1,0:T(8,128)(2,1)} %get-tuple-element.167), channel_id=1, source_target_pairs={{0,4},{1,5},{2,6},{3,7},{16,20},{17,21},{18,22},{19,23}} | collective-permute-start | bytes 1179656 | tf_op jit(solution)/shard_map/ppermute | solution.py:693
  392.5 19.1 %collective-permute-start.25 = (bf16[128,1536]{1,0:T(8,128)(2,1)S(1)}, bf16[128,1536]{1,0:T(8,128)(2,1)}, u32[]{:S(2)}, u32[]{:S(2)}) collective-permute-start(bf16[128,1536]{1,0:T(8,128)(2,1)S(1)} %get-tuple-element.166), channel_id=1, source_target_pairs={{12,8},{13,9},{14,10},{15,11},{28,24},{29,25},{30,26},{31,27}} | collective-permute-start | bytes 1179656 | tf_op jit(solution)/shard_map/ppermute | solution.py:694
  399.9 9.1 %copy-start.47 = (f32[128,1536]{1,0:T(8,128)S(1)}, f32[128,1536]{1,0:T(8,128)}, u32[]{:S(2)}) copy-start(f32[128,1536]{1,0:T(8,128)} %copy-done.45) | copy-start | bytes 2359300
  399.9 9.1 %copy-start.54 = (f32[128,1536]{1,0:T(8,128)S(1)}, f32[128,1536]{1,0:T(8,128)}, u32[]{:S(2)}) copy-start(f32[128,1536]{1,0:T(8,128)} %copy-done.53) | copy-start | bytes 2359300
  409.5 10.9 %copy-start.56 = (bf16[128,1536]{1,0:T(8,128)(2,1)S(1)}, bf16[128,1536]{1,0:T(8,128)(2,1)}, u32[]{:S(2)}) copy-start(bf16[128,1536]{1,0:T(8,128)(2,1)} %copy-done.55) | copy-start | bytes 1179652
  409.5 10.9 %copy-start.62 = (bf16[128,16]{1,0:T(8,128)(2,1)S(1)}, bf16[128,16]{1,0:T(8,128)(2,1)}, u32[]{:S(2)}) copy-start(bf16[128,16]{1,0:T(8,128)(2,1)} %copy-done.61) | copy-start | bytes 12292
  413.8 17.4 %collective-permute-start.26 = (bf16[128,1536]{1,0:T(8,128)(2,1)}, bf16[128,1536]{1,0:T(8,128)(2,1)}, u32[]{:S(2)}, u32[]{:S(2)}) collective-permute-start(bf16[128,1536]{1,0:T(8,128)(2,1)} %get-tuple-element.165), channel_id=1, source_target_pairs={{0,4},{4,8},{1,5},{5,9},{2,6},{6,10},{3,7},{7,11},{16,20},{20,24},... | collective-permute-start | bytes 1179656 | tf_op jit(solution)/shard_map/ppermute | solution.py:693
  418.9 12.3 %collective-permute-start.27 = (bf16[128,1536]{1,0:T(8,128)(2,1)}, bf16[128,1536]{1,0:T(8,128)(2,1)}, u32[]{:S(2)}, u32[]{:S(2)}) collective-permute-start(bf16[128,1536]{1,0:T(8,128)(2,1)} %get-tuple-element.164), channel_id=1, source_target_pairs={{12,8},{8,4},{13,9},{9,5},{14,10},{10,6},{15,11},{11,7},{28,24},{2... | collective-permute-start | bytes 1179656 | tf_op jit(solution)/shard_map/ppermute | solution.py:694
  426.7 4.5 copy-start.52
  426.7 25.4 %all-to-all-start.8 = ((bf16[4,8,48,384]{3,2,1,0:T(8,128)(2,1)}), bf16[4,8,48,384]{3,2,1,0:T(8,128)(2,1)}, u32[]{:S(2)}, u32[]{:S(2)}) async-start(bf16[4,8,48,384]{3,2,1,0:T(8,128)(2,1)} %shard_map.237), calls=%async_computation.8 | async-start | bytes 2359296 | tf_op jit(solution)/shard_map/all_to_all | solution.py:919
  431.1 39.4 %reduce-scatter.2.cloned.1.call-start = ((), (), s32[]{:S(2)}) async-start(), calls=%async_computation.13 | async-start | bytes 737280 | tf_op jit(solution)/shard_map/reduce_scatter | solution.py:904
  433.4 12.8 %collective-permute-start.28 = (bf16[128,1536]{1,0:T(8,128)(2,1)}, bf16[128,1536]{1,0:T(8,128)(2,1)}, u32[]{:S(2)}, u32[]{:S(2)}) collective-permute-start(bf16[128,1536]{1,0:T(8,128)(2,1)} %get-tuple-element.163), channel_id=1, source_target_pairs={{0,4},{4,8},{8,12},{1,5},{5,9},{9,13},{2,6},{6,10},{10,14},{3,7},{... | collective-permute-start | bytes 1179656 | tf_op jit(solution)/shard_map/ppermute | solution.py:693
  438.6 5.0 %copy-start.48 = (f32[128,1536]{1,0:T(8,128)S(1)}, f32[128,1536]{1,0:T(8,128)}, u32[]{:S(2)}) copy-start(f32[128,1536]{1,0:T(8,128)} %copy-done.45) | copy-start | bytes 2359300
  438.6 11.9 %collective-permute-start.29 = (bf16[128,1536]{1,0:T(8,128)(2,1)}, bf16[128,1536]{1,0:T(8,128)(2,1)}, u32[]{:S(2)}, u32[]{:S(2)}) collective-permute-start(bf16[128,1536]{1,0:T(8,128)(2,1)} %get-tuple-element.162), channel_id=1, source_target_pairs={{12,8},{8,4},{4,0},{13,9},{9,5},{5,1},{14,10},{10,6},{6,2},{15,11}... | collective-permute-start | bytes 1179656 | tf_op jit(solution)/shard_map/ppermute | solution.py:694
  443.6 7.0 %copy-start.12 = (bf16[128,1536]{1,0:T(8,128)(2,1)S(1)}, bf16[128,1536]{1,0:T(8,128)(2,1)}, u32[]{:S(2)}) copy-start(bf16[128,1536]{1,0:T(8,128)(2,1)} %refs_3_.1) | copy-start | bytes 1179652
  446.1 11.6 %copy-start.57 = (f32[128,1536]{1,0:T(8,128)S(1)}, f32[128,1536]{1,0:T(8,128)}, u32[]{:S(2)}) copy-start(f32[128,1536]{1,0:T(8,128)} %get-tuple-element.159) | copy-start | bytes 2359300
  454.3 13.4 %all-to-all-start.9 = ((bf16[8,48,384]{2,1,0:T(8,128)(2,1)}), bf16[8,48,384]{2,1,0:T(8,128)(2,1)S(1)}, u32[]{:S(2)}, u32[]{:S(2)}) async-start(bf16[8,48,384]{2,1,0:T(8,128)(2,1)} %reduce_sum.85), calls=%async_computation.9 | async-start | bytes 589824 | tf_op jit(solution)/shard_map/all_to_all | solution.py:921
  (44 other events, 59.2 us)
Sparse Core Ops, SparseCore 0:
  11.5 89.0 all-gather.2
  350.4 46.2 all-gather.4
  443.7 26.7 reduce-scatter.1
